TPU v7x, 128 devices: a whole 4x4x4 slice. The times are simulated.
128 devices in a mesh: pipe: 4 (over x), expert: 32 (over z, y, core).
Axes of the slice: x: 4, y: 4, z: 4, core: 2. Of those that a mesh axis runs over, the one named last changes fastest.
Arguments:
- inputs: bfloat16 [4, 1024, 3584], P(None, 'expert'), may hold values from -6 to 6
- cotangent: bfloat16 [4, 1024, 3584], P(None, 'expert'), may hold values from -6 to 6
- norm_gain: float32 [4, 3584], P('pipe'), may hold values from 0.5 to 1.5
- router_weight: bfloat16 [4, 3584, 16], P('pipe'), may hold values from -0.09375 to 0.09375
- gate_weight: bfloat16 [4, 3584, 16384], P('pipe', None, 'expert'), may hold values from -0.09375 to 0.09375
- up_weight: bfloat16 [4, 3584, 16384], P('pipe', None, 'expert'), may hold values from -0.09375 to 0.09375
- down_weight: bfloat16 [4, 16384, 3584], P('pipe', 'expert'), may hold values from -0.1875 to 0.1875
- route_ids: int32 [4, 4, 1024, 2], P('pipe', None, 'expert'), may hold values from 0 to 15, all different within a row; in each aligned block of 32 rows (0 to 31, 32 to 63, ..., all dimensions but the last counted through in order) at most 5 rows name the same one
Outputs:
- activations: bfloat16 [4, 4, 1024, 3584], P('pipe', None, 'expert')
- input_grads: bfloat16 [4, 4, 1024, 3584], P('pipe', None, 'expert')
Inputs may be any that keep to these rules, and one draw needn't show every extreme that they name: `route_ids`: in each aligned block of 32 rows (one device's tokens of one micro-batch at one section) every token names 2 different experts, no expert is named by more than 5 rows, and in some blocks an expert is named by exactly 5 rows.
All inputs are finite; a program needn't handle non-finite values.
Results may differ from a plain program's by a relative error of at most 0.03.
Values may be sent and summed in bfloat16 or wider, within the bound.
A program may use at most 128 MiB of HBM per device.

v0:
```python
import jax
import jax.numpy as jnp
from jax import lax
from jax.sharding import PartitionSpec as P

EPSILON = 1e-06


def for_sending(array):

    def short(part):
        return part.astype(jnp.bfloat16) if part.dtype == jnp.float32 else part

    return jax.tree.map(short, array)


def passed_along(block, axis, distance):
    devices = range(lax.axis_size(axis))
    route = [(i - distance, i) for i in devices if i - distance in devices]
    return lax.ppermute(block, axis, route)


def pick_micro(stacked, position):
    return lax.dynamic_index_in_dim(stacked, position, 0, keepdims=False)


def store_micro(stacked, position, values, enabled):
    previous = pick_micro(stacked, position)
    return lax.dynamic_update_index_in_dim(
        stacked, jnp.where(enabled, values, previous), position, 0
    )


def times_transposed(left_side, right_side):
    return lax.dot_general(
        left_side, right_side, (((1,), (1,)), ((), ())), preferred_element_type=jnp.float32
    )


def routing_tables(expert_ids, expert_count, capacity):
    token_count, top_count = expert_ids.shape
    expert_range = jnp.arange(expert_count, dtype=jnp.int32)
    one_hot = (expert_ids[:, :, None] == expert_range[None, None, :]).astype(jnp.int32)
    flat_hot = one_hot.reshape(token_count * top_count, expert_count)
    earlier = jnp.cumsum(flat_hot, axis=0) - flat_hot
    slot_index = jnp.sum(earlier * flat_hot, axis=1).reshape(token_count, top_count)
    target = expert_ids * capacity + slot_index
    slot_range = jnp.arange(expert_count * capacity, dtype=jnp.int32)
    pair_table = (target[:, :, None] == slot_range[None, None, :]).astype(jnp.bfloat16)
    token_table = jnp.sum(pair_table, axis=1)
    return (one_hot.astype(jnp.float32), pair_table, token_table)


def source_forward(layer_input, norm_scale, router, one_hot, token_table):
    input_wide = layer_input.astype(jnp.float32)
    scale_rows = lax.rsqrt(jnp.mean(input_wide * input_wide, axis=1, keepdims=True) + EPSILON)
    normed = (input_wide * scale_rows * norm_scale[None, :]).astype(jnp.bfloat16)
    logits = jnp.dot(normed, router, preferred_element_type=jnp.float32)
    scores = jnp.sum(logits[:, None, :] * one_hot, axis=2)
    probabilities = jax.nn.sigmoid(scores)
    totals = jnp.sum(probabilities, axis=1, keepdims=True)
    gate_values = probabilities / totals
    send_rows = lax.dot_general(
        token_table, normed, (((0,), (0,)), ((), ())), preferred_element_type=jnp.float32
    ).astype(jnp.bfloat16)
    return (scale_rows, gate_values, probabilities, totals, send_rows)


def finish_forward(layer_input, gate_values, pair_table, expert_out):
    picked = jnp.einsum("tkc,cd->tkd", pair_table, expert_out, preferred_element_type=jnp.float32)
    layer_output = layer_input.astype(jnp.float32) + jnp.sum(
        gate_values[:, :, None] * picked, axis=1
    )
    return (layer_output.astype(jnp.bfloat16), picked.astype(jnp.bfloat16))


def source_backward(grad_out, gate_values, pair_table):
    scaled = (gate_values[:, :, None] * grad_out.astype(jnp.float32)[:, None, :]).astype(
        jnp.bfloat16
    )
    return jnp.einsum("tkc,tkd->cd", pair_table, scaled, preferred_element_type=jnp.float32).astype(
        jnp.bfloat16
    )


def finish_backward(
    grad_out,
    layer_input,
    scale_rows,
    norm_scale,
    router,
    gate_values,
    probabilities,
    totals,
    picked,
    one_hot,
    token_table,
    back_rows,
):
    grad_wide = grad_out.astype(jnp.float32)
    gate_grad = jnp.einsum("tkd,td->tk", picked, grad_out, preferred_element_type=jnp.float32)
    weighted = jnp.sum(gate_values * gate_grad, axis=1, keepdims=True)
    score_grad = (gate_grad - weighted) / totals * probabilities * (1.0 - probabilities)
    router_table = jnp.sum(score_grad[:, :, None] * one_hot, axis=1).astype(jnp.bfloat16)
    router_part = times_transposed(router_table, router)
    expert_part = jnp.dot(token_table, back_rows, preferred_element_type=jnp.float32)
    normed_grad = (expert_part + router_part) * norm_scale[None, :]
    input_wide = layer_input.astype(jnp.float32)
    inner_term = jnp.mean(input_wide * normed_grad, axis=1, keepdims=True)
    result = grad_wide + scale_rows * normed_grad - input_wide * scale_rows**3 * inner_term
    return result.astype(jnp.bfloat16)


def expert_forward(rows_in, w_gate, w_up, w_down):
    gate_pre = jnp.dot(rows_in, w_gate, preferred_element_type=jnp.float32)
    up_pre = jnp.dot(rows_in, w_up, preferred_element_type=jnp.float32)
    hidden = (jax.nn.silu(gate_pre) * up_pre).astype(jnp.bfloat16)
    return (
        jnp.dot(hidden, w_down, preferred_element_type=jnp.float32).astype(jnp.bfloat16),
        gate_pre,
        up_pre,
    )


def expert_backward(rows_grad, gate_pre, up_pre, w_gate, w_up, w_down):
    hidden_grad = times_transposed(rows_grad, w_down)
    sigmoid_gate = jax.nn.sigmoid(gate_pre)
    pre_grad = (
        hidden_grad * up_pre * sigmoid_gate * (1.0 + gate_pre * (1.0 - sigmoid_gate))
    ).astype(jnp.bfloat16)
    up_grad = (hidden_grad * gate_pre * sigmoid_gate).astype(jnp.bfloat16)
    return (times_transposed(pre_grad, w_gate) + times_transposed(up_grad, w_up)).astype(
        jnp.bfloat16
    )


def dispatch_rows(send_rows):
    item_count, experts_here, capacity, model_width = send_rows.shape
    group_size = 2 * experts_here
    doubled = jnp.broadcast_to(
        send_rows[:, :, None], (item_count, experts_here, 2, capacity, model_width)
    )
    doubled = doubled.reshape(item_count, group_size, capacity, model_width)
    return lax.all_to_all(
        for_sending(doubled), "expert", split_axis=1, concat_axis=1, tiled=True
    ).astype(doubled.dtype)


def combine_rows(partial_value):
    item_count, group_size, capacity, model_width = partial_value.shape
    returned = lax.all_to_all(partial_value, "expert", split_axis=1, concat_axis=1, tiled=True)
    pair_sums = returned.reshape(item_count, group_size // 2, 2, capacity, model_width).astype(
        jnp.float32
    )
    return (pair_sums[:, :, 0] + pair_sums[:, :, 1]).astype(jnp.bfloat16)


def pass_forward(layer_output):
    return passed_along(layer_output, "pipe", 1)


def pass_backward(input_grad):
    return passed_along(input_grad, "pipe", -1)


def on_device(
    inputs, cotangent, norm_gain, router_weight, gate_weight, up_weight, down_weight, route_ids
):
    sections = lax.axis_size("pipe")
    section_index = lax.axis_index("pipe")
    group_size = lax.axis_size("expert")
    micro_count, tokens_here, model_width = inputs.shape
    experts_here = router_weight.shape[2]
    top_count = route_ids.shape[3]
    capacity = min(
        tokens_here, (5 * tokens_here * top_count + 4 * experts_here - 1) // (4 * experts_here)
    )
    rows_total = group_size * capacity
    norm_scale = norm_gain[0]
    router = router_weight[0]
    w_gate = gate_weight[0]
    w_up = up_weight[0]
    w_down = down_weight[0]
    all_ids = route_ids[0]
    hidden_here = w_gate.shape[1]
    zero_tokens = jnp.zeros((micro_count, tokens_here, model_width), jnp.bfloat16)
    saved = dict(
        inputs=zero_tokens,
        scale=jnp.zeros((micro_count, tokens_here, 1), jnp.float32),
        gates=jnp.zeros((micro_count, tokens_here, top_count), jnp.float32),
        probs=jnp.zeros((micro_count, tokens_here, top_count), jnp.float32),
        totals=jnp.zeros((micro_count, tokens_here, 1), jnp.float32),
        picked=jnp.zeros((micro_count, tokens_here, top_count, model_width), jnp.bfloat16),
        gate_pre=jnp.zeros((micro_count, rows_total, hidden_here), jnp.float32),
        up_pre=jnp.zeros((micro_count, rows_total, hidden_here), jnp.float32),
    )
    forward_out = zero_tokens
    backward_out = zero_tokens

    def record(stash, micro_index, enabled, fresh):
        return {
            entry: store_micro(stash[entry], micro_index, fresh[entry], enabled) for entry in stash
        }

    def backward_prepare(stash, micro_index, received):
        grad_out = jnp.where(
            section_index == sections - 1, pick_micro(cotangent, micro_index), received
        )
        one_hot, pair_table, token_table = routing_tables(
            pick_micro(all_ids, micro_index), experts_here, capacity
        )
        kept = {entry: pick_micro(stash[entry], micro_index) for entry in stash}
        send_rows = source_backward(grad_out, kept["gates"], pair_table)
        return dict(
            grad_out=grad_out,
            one_hot=one_hot,
            token_table=token_table,
            kept=kept,
            send_rows=send_rows.reshape(experts_here, capacity, model_width),
        )

    received_fwd = jnp.zeros((tokens_here, model_width), jnp.bfloat16)
    received_bwd = jnp.zeros((tokens_here, model_width), jnp.bfloat16)
    for tick_index in range(micro_count + sections - 1):
        offset_fwd = tick_index - section_index
        micro_fwd = jnp.clip(offset_fwd, 0, micro_count - 1)
        enabled_fwd = (offset_fwd >= 0) & (offset_fwd < micro_count)
        layer_input = jnp.where(section_index == 0, pick_micro(inputs, micro_fwd), received_fwd)
        forward_one_hot, forward_pair_table, forward_token_table = routing_tables(
            pick_micro(all_ids, micro_fwd), experts_here, capacity
        )
        scale_rows, gate_values, probabilities, totals, forward_send_rows = source_forward(
            layer_input, norm_scale, router, forward_one_hot, forward_token_table
        )
        prep = dict(
            layer_input=layer_input,
            scale=scale_rows,
            gates=gate_values,
            probs=probabilities,
            totals=totals,
            pair_table=forward_pair_table,
            send_rows=forward_send_rows.reshape(experts_here, capacity, model_width),
        )
        arrived = dispatch_rows(prep["send_rows"][None])
        partial_fwd, gate_pre, up_pre = expert_forward(
            arrived[0].reshape(rows_total, model_width), w_gate, w_up, w_down
        )
        returned = combine_rows(partial_fwd.reshape(1, group_size, capacity, model_width))
        layer_output, picked = finish_forward(
            prep["layer_input"],
            prep["gates"],
            prep["pair_table"],
            returned[0].reshape(experts_here * capacity, model_width),
        )
        forward_fresh = dict(
            inputs=prep["layer_input"],
            scale=prep["scale"],
            gates=prep["gates"],
            probs=prep["probs"],
            totals=prep["totals"],
            picked=picked,
            gate_pre=gate_pre,
            up_pre=up_pre,
        )
        layer_output, fresh = (layer_output, forward_fresh)
        saved = record(saved, micro_fwd, enabled_fwd, fresh)
        forward_out = store_micro(forward_out, micro_fwd, layer_output, enabled_fwd)
        received_fwd = pass_forward(layer_output)
    for tick_index in range(micro_count + sections - 1):
        offset_bwd = tick_index - (sections - 1 - section_index)
        micro_bwd = jnp.clip(offset_bwd, 0, micro_count - 1)
        enabled_bwd = (offset_bwd >= 0) & (offset_bwd < micro_count)
        back_prep = backward_prepare(saved, micro_bwd, received_bwd)
        arrived = dispatch_rows(back_prep["send_rows"][None])
        kept = back_prep["kept"]
        partial_bwd = expert_backward(
            arrived[0].reshape(rows_total, model_width),
            kept["gate_pre"],
            kept["up_pre"],
            w_gate,
            w_up,
            w_down,
        )
        returned = combine_rows(partial_bwd.reshape(1, group_size, capacity, model_width))
        backward_returned = returned[0]
        backward_kept = back_prep["kept"]
        input_grad = finish_backward(
            back_prep["grad_out"],
            backward_kept["inputs"],
            backward_kept["scale"],
            norm_scale,
            router,
            backward_kept["gates"],
            backward_kept["probs"],
            backward_kept["totals"],
            backward_kept["picked"],
            back_prep["one_hot"],
            back_prep["token_table"],
            backward_returned.reshape(experts_here * capacity, model_width),
        )
        backward_out = store_micro(backward_out, micro_bwd, input_grad, enabled_bwd)
        received_bwd = pass_backward(input_grad)
    return (forward_out[None], backward_out[None])


def solution(mesh):
    return jax.shard_map(
        on_device,
        mesh=mesh,
        in_specs=(
            P(None, "expert", None),
            P(None, "expert", None),
            P("pipe", None),
            P("pipe", None, None),
            P("pipe", None, "expert"),
            P("pipe", None, "expert"),
            P("pipe", "expert", None),
            P("pipe", None, "expert", None),
        ),
        out_specs=(P("pipe", None, "expert", None), P("pipe", None, "expert", None)),
        check_vma=False,
    )
```

profile of v0, /device:TPU:1, one launch (start us, length us, event | category | flops | bytes accessed | tf_op | source)
XLA Modules:
  0.0 1409.5 jit_solution(4977007750263985402)
XLA Ops:
  8.0 9.7 all-to-all-start
  30.2 12.4 all-to-all-done
  67.0 20.0 %all-to-all-done.1 = bf16[1,32,5,3584]{3,2,0,1:T(8,128)(2,1)} async-done(((bf16[1,32,5,3584]{3,2,0,1:T(8,128)(2,1)}), bf16[1,32,5,3584]{3,2,0,1:T(8,128)(2,1)}, u32[]{:S(2)}, u32[]{:S(2)}) %all-to-all-start.1) | async-done | bytes 1146912 | tf_op jit(solution)/shard_map/all_to_all | solution.py:151
  105.9 7.9 all-to-all-start.2
  116.5 22.0 %all-to-all-done.2 = bf16[1,32,5,3584]{3,2,0,1:T(8,128)(2,1)} async-done(((bf16[1,32,5,3584]{3,2,0,1:T(8,128)(2,1)}), bf16[1,32,5,3584]{3,2,0,1:T(8,128)(2,1)}, u32[]{:S(2)}, u32[]{:S(2)}) %all-to-all-start.2) | async-done | bytes 1146912 | tf_op jit(solution)/shard_map/all_to_all | solution.py:144
  163.9 19.3 %all-to-all-done.3 = bf16[1,32,5,3584]{3,2,0,1:T(8,128)(2,1)} async-done(((bf16[1,32,5,3584]{3,2,0,1:T(8,128)(2,1)}), bf16[1,32,5,3584]{3,2,0,1:T(8,128)(2,1)}, u32[]{:S(2)}, u32[]{:S(2)}) %all-to-all-start.3) | async-done | bytes 1146912 | tf_op jit(solution)/shard_map/all_to_all | solution.py:151
  207.7 7.5 all-to-all-start.4
  219.7 20.6 %all-to-all-done.4 = bf16[1,32,5,3584]{3,2,0,1:T(8,128)(2,1)} async-done(((bf16[1,32,5,3584]{3,2,0,1:T(8,128)(2,1)}), bf16[1,32,5,3584]{3,2,0,1:T(8,128)(2,1)}, u32[]{:S(2)}, u32[]{:S(2)}) %all-to-all-start.4) | async-done | bytes 1146912 | tf_op jit(solution)/shard_map/all_to_all | solution.py:144
  265.3 19.6 %all-to-all-done.5 = bf16[1,32,5,3584]{3,2,0,1:T(8,128)(2,1)} async-done(((bf16[1,32,5,3584]{3,2,0,1:T(8,128)(2,1)}), bf16[1,32,5,3584]{3,2,0,1:T(8,128)(2,1)}, u32[]{:S(2)}, u32[]{:S(2)}) %all-to-all-start.5) | async-done | bytes 1146912 | tf_op jit(solution)/shard_map/all_to_all | solution.py:151
  309.3 7.9 all-to-all-start.6
  322.1 19.9 %all-to-all-done.6 = bf16[1,32,5,3584]{3,2,0,1:T(8,128)(2,1)} async-done(((bf16[1,32,5,3584]{3,2,0,1:T(8,128)(2,1)}), bf16[1,32,5,3584]{3,2,0,1:T(8,128)(2,1)}, u32[]{:S(2)}, u32[]{:S(2)}) %all-to-all-start.6) | async-done | bytes 1146912 | tf_op jit(solution)/shard_map/all_to_all | solution.py:144
  367.1 19.6 %all-to-all-done.7 = bf16[1,32,5,3584]{3,2,0,1:T(8,128)(2,1)} async-done(((bf16[1,32,5,3584]{3,2,0,1:T(8,128)(2,1)}), bf16[1,32,5,3584]{3,2,0,1:T(8,128)(2,1)}, u32[]{:S(2)}, u32[]{:S(2)}) %all-to-all-start.7) | async-done | bytes 1146912 | tf_op jit(solution)/shard_map/all_to_all | solution.py:151
  411.3 7.5 all-to-all-start.8
  422.7 21.1 %all-to-all-done.8 = bf16[1,32,5,3584]{3,2,0,1:T(8,128)(2,1)} async-done(((bf16[1,32,5,3584]{3,2,0,1:T(8,128)(2,1)}), bf16[1,32,5,3584]{3,2,0,1:T(8,128)(2,1)}, u32[]{:S(2)}, u32[]{:S(2)}) %all-to-all-start.8) | async-done | bytes 1146912 | tf_op jit(solution)/shard_map/all_to_all | solution.py:144
  466.4 22.0 %all-to-all-done.9 = bf16[1,32,5,3584]{3,2,0,1:T(8,128)(2,1)} async-done(((bf16[1,32,5,3584]{3,2,0,1:T(8,128)(2,1)}), bf16[1,32,5,3584]{3,2,0,1:T(8,128)(2,1)}, u32[]{:S(2)}, u32[]{:S(2)}) %all-to-all-start.9) | async-done | bytes 1146912 | tf_op jit(solution)/shard_map/all_to_all | solution.py:151
  513.6 8.1 all-to-all-start.10
  523.7 22.8 %all-to-all-done.10 = bf16[1,32,5,3584]{3,2,0,1:T(8,128)(2,1)} async-done(((bf16[1,32,5,3584]{3,2,0,1:T(8,128)(2,1)}), bf16[1,32,5,3584]{3,2,0,1:T(8,128)(2,1)}, u32[]{:S(2)}, u32[]{:S(2)}) %all-to-all-start.10) | async-done | bytes 1146912 | tf_op jit(solution)/shard_map/all_to_all | solution.py:144
  559.5 6.7 all-to-all-start.11
  570.9 20.3 %all-to-all-done.11 = bf16[1,32,5,3584]{3,2,0,1:T(8,128)(2,1)} async-done(((bf16[1,32,5,3584]{3,2,0,1:T(8,128)(2,1)}), bf16[1,32,5,3584]{3,2,0,1:T(8,128)(2,1)}, u32[]{:S(2)}, u32[]{:S(2)}) %all-to-all-start.11) | async-done | bytes 1146912 | tf_op jit(solution)/shard_map/all_to_all | solution.py:151
  616.4 7.5 all-to-all-start.12
  627.4 21.4 %all-to-all-done.12 = bf16[1,32,5,3584]{3,2,0,1:T(8,128)(2,1)} async-done(((bf16[1,32,5,3584]{3,2,0,1:T(8,128)(2,1)}), bf16[1,32,5,3584]{3,2,0,1:T(8,128)(2,1)}, u32[]{:S(2)}, u32[]{:S(2)}) %all-to-all-start.12) | async-done | bytes 1146912 | tf_op jit(solution)/shard_map/all_to_all | solution.py:144
  671.4 22.1 %all-to-all-done.13 = bf16[1,32,5,3584]{3,2,0,1:T(8,128)(2,1)} async-done(((bf16[1,32,5,3584]{3,2,0,1:T(8,128)(2,1)}), bf16[1,32,5,3584]{3,2,0,1:T(8,128)(2,1)}, u32[]{:S(2)}, u32[]{:S(2)}) %all-to-all-start.13) | async-done | bytes 1146912 | tf_op jit(solution)/shard_map/all_to_all | solution.py:151
  717.2 21.6 %all-to-all-done.14 = bf16[1,32,5,3584]{3,2,0,1:T(8,128)(2,1)S(1)} async-done(((bf16[1,32,5,3584]{3,2,0,1:T(8,128)(2,1)}), bf16[1,32,5,3584]{3,2,0,1:T(8,128)(2,1)S(1)}, u32[]{:S(2)}, u32[]{:S(2)}) %all-to-all-start.14) | async-done | bytes 1146912 | tf_op jit(solution)/shard_map/all_to_all | solution.py:144
  750.9 6.7 all-to-all-start.15
  759.2 23.4 %all-to-all-done.15 = bf16[1,32,5,3584]{3,2,0,1:T(8,128)(2,1)} async-done(((bf16[1,32,5,3584]{3,2,0,1:T(8,128)(2,1)}), bf16[1,32,5,3584]{3,2,0,1:T(8,128)(2,1)}, u32[]{:S(2)}, u32[]{:S(2)}) %all-to-all-start.15) | async-done | bytes 1146912 | tf_op jit(solution)/shard_map/all_to_all | solution.py:151
  810.0 7.5 all-to-all-start.16
  817.5 25.0 %all-to-all-done.16 = bf16[1,32,5,3584]{3,2,0,1:T(8,128)(2,1)} async-done(((bf16[1,32,5,3584]{3,2,0,1:T(8,128)(2,1)}), bf16[1,32,5,3584]{3,2,0,1:T(8,128)(2,1)}, u32[]{:S(2)}, u32[]{:S(2)}) %all-to-all-start.16) | async-done | bytes 1146912 | tf_op jit(solution)/shard_map/all_to_all | solution.py:144
  855.9 6.7 all-to-all-start.17
  864.6 23.0 %all-to-all-done.17 = bf16[1,32,5,3584]{3,2,0,1:T(8,128)(2,1)} async-done(((bf16[1,32,5,3584]{3,2,0,1:T(8,128)(2,1)}), bf16[1,32,5,3584]{3,2,0,1:T(8,128)(2,1)}, u32[]{:S(2)}, u32[]{:S(2)}) %all-to-all-start.17) | async-done | bytes 1146912 | tf_op jit(solution)/shard_map/all_to_all | solution.py:151
  914.0 7.6 all-to-all-start.18
  922.4 24.3 %all-to-all-done.18 = bf16[1,32,5,3584]{3,2,0,1:T(8,128)(2,1)} async-done(((bf16[1,32,5,3584]{3,2,0,1:T(8,128)(2,1)}), bf16[1,32,5,3584]{3,2,0,1:T(8,128)(2,1)}, u32[]{:S(2)}, u32[]{:S(2)}) %all-to-all-start.18) | async-done | bytes 1146912 | tf_op jit(solution)/shard_map/all_to_all | solution.py:144
  960.0 6.7 all-to-all-start.19
  968.8 23.0 %all-to-all-done.19 = bf16[1,32,5,3584]{3,2,0,1:T(8,128)(2,1)} async-done(((bf16[1,32,5,3584]{3,2,0,1:T(8,128)(2,1)}), bf16[1,32,5,3584]{3,2,0,1:T(8,128)(2,1)}, u32[]{:S(2)}, u32[]{:S(2)}) %all-to-all-start.19) | async-done | bytes 1146912 | tf_op jit(solution)/shard_map/all_to_all | solution.py:151
  1017.7 7.5 all-to-all-start.20
  1025.2 25.0 %all-to-all-done.20 = bf16[1,32,5,3584]{3,2,0,1:T(8,128)(2,1)} async-done(((bf16[1,32,5,3584]{3,2,0,1:T(8,128)(2,1)}), bf16[1,32,5,3584]{3,2,0,1:T(8,128)(2,1)}, u32[]{:S(2)}, u32[]{:S(2)}) %all-to-all-start.20) | async-done | bytes 1146912 | tf_op jit(solution)/shard_map/all_to_all | solution.py:144
  1063.6 7.1 all-to-all-start.21
  1072.8 23.0 %all-to-all-done.21 = bf16[1,32,5,3584]{3,2,0,1:T(8,128)(2,1)} async-done(((bf16[1,32,5,3584]{3,2,0,1:T(8,128)(2,1)}), bf16[1,32,5,3584]{3,2,0,1:T(8,128)(2,1)}, u32[]{:S(2)}, u32[]{:S(2)}) %all-to-all-start.21) | async-done | bytes 1146912 | tf_op jit(solution)/shard_map/all_to_all | solution.py:151
  1122.2 7.6 all-to-all-start.22
  1130.6 24.3 %all-to-all-done.22 = bf16[1,32,5,3584]{3,2,0,1:T(8,128)(2,1)} async-done(((bf16[1,32,5,3584]{3,2,0,1:T(8,128)(2,1)}), bf16[1,32,5,3584]{3,2,0,1:T(8,128)(2,1)}, u32[]{:S(2)}, u32[]{:S(2)}) %all-to-all-start.22) | async-done | bytes 1146912 | tf_op jit(solution)/shard_map/all_to_all | solution.py:144
  1168.2 6.7 all-to-all-start.23
  1177.0 23.0 %all-to-all-done.23 = bf16[1,32,5,3584]{3,2,0,1:T(8,128)(2,1)} async-done(((bf16[1,32,5,3584]{3,2,0,1:T(8,128)(2,1)}), bf16[1,32,5,3584]{3,2,0,1:T(8,128)(2,1)}, u32[]{:S(2)}, u32[]{:S(2)}) %all-to-all-start.23) | async-done | bytes 1146912 | tf_op jit(solution)/shard_map/all_to_all | solution.py:151
  1225.9 7.8 all-to-all-start.24
  1233.8 24.8 %all-to-all-done.24 = bf16[1,32,5,3584]{3,2,0,1:T(8,128)(2,1)} async-done(((bf16[1,32,5,3584]{3,2,0,1:T(8,128)(2,1)}), bf16[1,32,5,3584]{3,2,0,1:T(8,128)(2,1)}, u32[]{:S(2)}, u32[]{:S(2)}) %all-to-all-start.24) | async-done | bytes 1146912 | tf_op jit(solution)/shard_map/all_to_all | solution.py:144
  1271.9 6.8 all-to-all-start.25
  1280.8 23.0 %all-to-all-done.25 = bf16[1,32,5,3584]{3,2,0,1:T(8,128)(2,1)} async-done(((bf16[1,32,5,3584]{3,2,0,1:T(8,128)(2,1)}), bf16[1,32,5,3584]{3,2,0,1:T(8,128)(2,1)}, u32[]{:S(2)}, u32[]{:S(2)}) %all-to-all-start.25) | async-done | bytes 1146912 | tf_op jit(solution)/shard_map/all_to_all | solution.py:151
  1329.7 7.5 all-to-all-start.26
  1339.4 22.8 %all-to-all-done.26 = bf16[1,32,5,3584]{3,2,0,1:T(8,128)(2,1)} async-done(((bf16[1,32,5,3584]{3,2,0,1:T(8,128)(2,1)}), bf16[1,32,5,3584]{3,2,0,1:T(8,128)(2,1)}, u32[]{:S(2)}, u32[]{:S(2)}) %all-to-all-start.26) | async-done | bytes 1146912 | tf_op jit(solution)/shard_map/all_to_all | solution.py:144
  1384.5 20.1 %all-to-all-done.27 = bf16[1,32,5,3584]{3,2,0,1:T(8,128)(2,1)S(1)} async-done(((bf16[1,32,5,3584]{3,2,0,1:T(8,128)(2,1)}), bf16[1,32,5,3584]{3,2,0,1:T(8,128)(2,1)S(1)}, u32[]{:S(2)}, u32[]{:S(2)}) %all-to-all-start.27) | async-done | bytes 1146912 | tf_op jit(solution)/shard_map/all_to_all | solution.py:151
  (833 shorter events, 648.1 us)
Async XLA Ops:
  2.3 19.3 %copy-start.87 = (s32[1,1,32,2]{2,3,1,0:T(2,128)}, s32[1,1,32,2]{2,3,1,0:T(2,128)S(1)}, u32[]{:S(2)}) copy-start(s32[1,1,32,2]{2,3,1,0:T(2,128)S(1)} %get-tuple-element.95) | copy-start | bytes 772
  2.3 21.1 %copy-start.86 = (s32[1,1,32,2]{2,3,1,0:T(2,128)}, s32[1,1,32,2]{2,3,1,0:T(2,128)S(1)}, u32[]{:S(2)}) copy-start(s32[1,1,32,2]{2,3,1,0:T(2,128)S(1)} %get-tuple-element.94) | copy-start | bytes 772
  2.3 22.0 %copy-start.85 = (s32[1,1,32,2]{2,3,1,0:T(2,128)}, s32[1,1,32,2]{2,3,1,0:T(2,128)S(1)}, u32[]{:S(2)}) copy-start(s32[1,1,32,2]{2,3,1,0:T(2,128)S(1)} %get-tuple-element.93) | copy-start | bytes 772
  2.3 23.9 %copy-start.84 = (s32[1,1,32,2]{2,3,1,0:T(2,128)}, s32[1,1,32,2]{2,3,1,0:T(2,128)S(1)}, u32[]{:S(2)}) copy-start(s32[1,1,32,2]{2,3,1,0:T(2,128)S(1)} %get-tuple-element.92) | copy-start | bytes 772
  2.3 24.7 %copy-start.96 = (s32[1,1,32,2]{2,3,1,0:T(2,128)}, s32[1,1,32,2]{2,3,1,0:T(2,128)S(1)}, u32[]{:S(2)}) copy-start(s32[1,1,32,2]{2,3,1,0:T(2,128)S(1)} %get-tuple-element.90) | copy-start | bytes 772
  2.3 25.1 %copy-start.94 = (s32[1,1,32,2]{2,3,1,0:T(2,128)}, s32[1,1,32,2]{2,3,1,0:T(2,128)S(1)}, u32[]{:S(2)}) copy-start(s32[1,1,32,2]{2,3,1,0:T(2,128)S(1)} %get-tuple-element.89) | copy-start | bytes 772
  2.3 26.1 %copy-start.98 = (s32[1,1,32,2]{2,3,1,0:T(2,128)}, s32[1,1,32,2]{2,3,1,0:T(2,128)S(1)}, u32[]{:S(2)}) copy-start(s32[1,1,32,2]{2,3,1,0:T(2,128)S(1)} %get-tuple-element.91) | copy-start | bytes 772
  8.0 34.6 %all-to-all-start = ((bf16[1,32,5,3584]{3,2,0,1:T(8,128)(2,1)}), bf16[1,32,5,3584]{3,2,0,1:T(8,128)(2,1)S(1)}, u32[]{:S(2)}, u32[]{:S(2)}) async-start(bf16[1,32,5,3584]{3,2,0,1:T(8,128)(2,1)} %bitcast.1324), calls=%async_computation | async-start | bytes 3670016 | tf_op jit(solution)/shard_map/all_to_all | solution.py:144
  28.4 33.4 %copy-start.107 = (s32[32,2]{0,1:T(2,128)}, s32[32,2]{0,1:T(2,128)S(1)}, u32[]{:S(2)}) copy-start(s32[32,2]{0,1:T(2,128)S(1)} %multiply_add_fusion.6) | copy-start | bytes 772
  55.3 31.6 %all-to-all-start.1 = ((bf16[1,32,5,3584]{3,2,0,1:T(8,128)(2,1)}), bf16[1,32,5,3584]{3,2,0,1:T(8,128)(2,1)}, u32[]{:S(2)}, u32[]{:S(2)}) async-start(bf16[1,32,5,3584]{3,2,0,1:T(8,128)(2,1)} %bitcast.1341), calls=%async_computation.1 | async-start | bytes 3670016 | tf_op jit(solution)/shard_map/all_to_all | solution.py:151
  90.7 6.1 collective-permute-start
  105.9 32.6 %all-to-all-start.2 = ((bf16[1,32,5,3584]{3,2,0,1:T(8,128)(2,1)}), bf16[1,32,5,3584]{3,2,0,1:T(8,128)(2,1)}, u32[]{:S(2)}, u32[]{:S(2)}) async-start(bf16[1,32,5,3584]{3,2,0,1:T(8,128)(2,1)} %bitcast.1327), calls=%async_computation.2 | async-start | bytes 3670016 | tf_op jit(solution)/shard_map/all_to_all | solution.py:144
  151.5 31.7 %all-to-all-start.3 = ((bf16[1,32,5,3584]{3,2,0,1:T(8,128)(2,1)}), bf16[1,32,5,3584]{3,2,0,1:T(8,128)(2,1)}, u32[]{:S(2)}, u32[]{:S(2)}) async-start(bf16[1,32,5,3584]{3,2,0,1:T(8,128)(2,1)} %bitcast.1345), calls=%async_computation.3 | async-start | bytes 3670016 | tf_op jit(solution)/shard_map/all_to_all | solution.py:151
  191.8 7.0 collective-permute-start.1
  207.7 32.5 %all-to-all-start.4 = ((bf16[1,32,5,3584]{3,2,0,1:T(8,128)(2,1)}), bf16[1,32,5,3584]{3,2,0,1:T(8,128)(2,1)}, u32[]{:S(2)}, u32[]{:S(2)}) async-start(bf16[1,32,5,3584]{3,2,0,1:T(8,128)(2,1)} %bitcast.1339), calls=%async_computation.4 | async-start | bytes 3670016 | tf_op jit(solution)/shard_map/all_to_all | solution.py:144
  253.2 31.7 %all-to-all-start.5 = ((bf16[1,32,5,3584]{3,2,0,1:T(8,128)(2,1)}), bf16[1,32,5,3584]{3,2,0,1:T(8,128)(2,1)}, u32[]{:S(2)}, u32[]{:S(2)}) async-start(bf16[1,32,5,3584]{3,2,0,1:T(8,128)(2,1)} %bitcast.1330), calls=%async_computation.5 | async-start | bytes 3670016 | tf_op jit(solution)/shard_map/all_to_all | solution.py:151
  293.4 7.0 collective-permute-start.2
  309.3 32.7 %all-to-all-start.6 = ((bf16[1,32,5,3584]{3,2,0,1:T(8,128)(2,1)}), bf16[1,32,5,3584]{3,2,0,1:T(8,128)(2,1)}, u32[]{:S(2)}, u32[]{:S(2)}) async-start(bf16[1,32,5,3584]{3,2,0,1:T(8,128)(2,1)} %bitcast.1342), calls=%async_computation.6 | async-start | bytes 3670016 | tf_op jit(solution)/shard_map/all_to_all | solution.py:144
  355.0 31.7 %all-to-all-start.7 = ((bf16[1,32,5,3584]{3,2,0,1:T(8,128)(2,1)}), bf16[1,32,5,3584]{3,2,0,1:T(8,128)(2,1)}, u32[]{:S(2)}, u32[]{:S(2)}) async-start(bf16[1,32,5,3584]{3,2,0,1:T(8,128)(2,1)} %bitcast.1331), calls=%async_computation.7 | async-start | bytes 3670016 | tf_op jit(solution)/shard_map/all_to_all | solution.py:151
  395.3 7.1 collective-permute-start.3
  411.3 32.5 %all-to-all-start.8 = ((bf16[1,32,5,3584]{3,2,0,1:T(8,128)(2,1)}), bf16[1,32,5,3584]{3,2,0,1:T(8,128)(2,1)}, u32[]{:S(2)}, u32[]{:S(2)}) async-start(bf16[1,32,5,3584]{3,2,0,1:T(8,128)(2,1)} %bitcast.1350), calls=%async_computation.8 | async-start | bytes 3670016 | tf_op jit(solution)/shard_map/all_to_all | solution.py:144
  456.7 31.6 %all-to-all-start.9 = ((bf16[1,32,5,3584]{3,2,0,1:T(8,128)(2,1)}), bf16[1,32,5,3584]{3,2,0,1:T(8,128)(2,1)}, u32[]{:S(2)}, u32[]{:S(2)}) async-start(bf16[1,32,5,3584]{3,2,0,1:T(8,128)(2,1)} %bitcast.1333), calls=%async_computation.9 | async-start | bytes 3670016 | tf_op jit(solution)/shard_map/all_to_all | solution.py:151
  497.7 7.0 collective-permute-start.4
  513.6 32.9 %all-to-all-start.10 = ((bf16[1,32,5,3584]{3,2,0,1:T(8,128)(2,1)}), bf16[1,32,5,3584]{3,2,0,1:T(8,128)(2,1)}, u32[]{:S(2)}, u32[]{:S(2)}) async-start(bf16[1,32,5,3584]{3,2,0,1:T(8,128)(2,1)} %bitcast.1346), calls=%async_computation.10 | async-start | bytes 3670016 | tf_op jit(solution)/shard_map/all_to_all | solution.py:144
  559.5 31.7 %all-to-all-start.11 = ((bf16[1,32,5,3584]{3,2,0,1:T(8,128)(2,1)}), bf16[1,32,5,3584]{3,2,0,1:T(8,128)(2,1)}, u32[]{:S(2)}, u32[]{:S(2)}) async-start(bf16[1,32,5,3584]{3,2,0,1:T(8,128)(2,1)} %bitcast.1343), calls=%async_computation.11 | async-start | bytes 3670016 | tf_op jit(solution)/shard_map/all_to_all | solution.py:151
  600.4 7.1 collective-permute-start.5
  616.4 32.5 %all-to-all-start.12 = ((bf16[1,32,5,3584]{3,2,0,1:T(8,128)(2,1)}), bf16[1,32,5,3584]{3,2,0,1:T(8,128)(2,1)}, u32[]{:S(2)}, u32[]{:S(2)}) async-start(bf16[1,32,5,3584]{3,2,0,1:T(8,128)(2,1)} %bitcast.1344), calls=%async_computation.12 | async-start | bytes 3670016 | tf_op jit(solution)/shard_map/all_to_all | solution.py:144
  661.8 31.7 %all-to-all-start.13 = ((bf16[1,32,5,3584]{3,2,0,1:T(8,128)(2,1)}), bf16[1,32,5,3584]{3,2,0,1:T(8,128)(2,1)}, u32[]{:S(2)}, u32[]{:S(2)}) async-start(bf16[1,32,5,3584]{3,2,0,1:T(8,128)(2,1)} %bitcast.1332), calls=%async_computation.13 | async-start | bytes 3670016 | tf_op jit(solution)/shard_map/all_to_all | solution.py:151
  707.7 31.1 %all-to-all-start.14 = ((bf16[1,32,5,3584]{3,2,0,1:T(8,128)(2,1)}), bf16[1,32,5,3584]{3,2,0,1:T(8,128)(2,1)S(1)}, u32[]{:S(2)}, u32[]{:S(2)}) async-start(bf16[1,32,5,3584]{3,2,0,1:T(8,128)(2,1)} %bitcast.1326), calls=%async_computation.14 | async-start | bytes 3670016 | tf_op jit(solution)/shard_map/all_to_all | solution.py:144
  750.9 31.7 %all-to-all-start.15 = ((bf16[1,32,5,3584]{3,2,0,1:T(8,128)(2,1)}), bf16[1,32,5,3584]{3,2,0,1:T(8,128)(2,1)}, u32[]{:S(2)}, u32[]{:S(2)}) async-start(bf16[1,32,5,3584]{3,2,0,1:T(8,128)(2,1)} %bitcast.1325), calls=%async_computation.15 | async-start | bytes 3670016 | tf_op jit(solution)/shard_map/all_to_all | solution.py:151
  792.3 7.6 collective-permute-start.6
  810.0 32.5 %all-to-all-start.16 = ((bf16[1,32,5,3584]{3,2,0,1:T(8,128)(2,1)}), bf16[1,32,5,3584]{3,2,0,1:T(8,128)(2,1)}, u32[]{:S(2)}, u32[]{:S(2)}) async-start(bf16[1,32,5,3584]{3,2,0,1:T(8,128)(2,1)} %bitcast.1347), calls=%async_computation.16 | async-start | bytes 3670016 | tf_op jit(solution)/shard_map/all_to_all | solution.py:144
  855.9 31.8 %all-to-all-start.17 = ((bf16[1,32,5,3584]{3,2,0,1:T(8,128)(2,1)}), bf16[1,32,5,3584]{3,2,0,1:T(8,128)(2,1)}, u32[]{:S(2)}, u32[]{:S(2)}) async-start(bf16[1,32,5,3584]{3,2,0,1:T(8,128)(2,1)} %bitcast.1334), calls=%async_computation.17 | async-start | bytes 3670016 | tf_op jit(solution)/shard_map/all_to_all | solution.py:151
  896.4 7.1 collective-permute-start.7
  914.0 32.6 %all-to-all-start.18 = ((bf16[1,32,5,3584]{3,2,0,1:T(8,128)(2,1)}), bf16[1,32,5,3584]{3,2,0,1:T(8,128)(2,1)}, u32[]{:S(2)}, u32[]{:S(2)}) async-start(bf16[1,32,5,3584]{3,2,0,1:T(8,128)(2,1)} %bitcast.1329), calls=%async_computation.18 | async-start | bytes 3670016 | tf_op jit(solution)/shard_map/all_to_all | solution.py:144
  960.0 31.8 %all-to-all-start.19 = ((bf16[1,32,5,3584]{3,2,0,1:T(8,128)(2,1)}), bf16[1,32,5,3584]{3,2,0,1:T(8,128)(2,1)}, u32[]{:S(2)}, u32[]{:S(2)}) async-start(bf16[1,32,5,3584]{3,2,0,1:T(8,128)(2,1)} %bitcast.1335), calls=%async_computation.19 | async-start | bytes 3670016 | tf_op jit(solution)/shard_map/all_to_all | solution.py:151
  1000.6 7.1 collective-permute-start.8
  1017.7 32.5 %all-to-all-start.20 = ((bf16[1,32,5,3584]{3,2,0,1:T(8,128)(2,1)}), bf16[1,32,5,3584]{3,2,0,1:T(8,128)(2,1)}, u32[]{:S(2)}, u32[]{:S(2)}) async-start(bf16[1,32,5,3584]{3,2,0,1:T(8,128)(2,1)} %bitcast.1348), calls=%async_computation.20 | async-start | bytes 3670016 | tf_op jit(solution)/shard_map/all_to_all | solution.py:144
  1063.6 32.2 %all-to-all-start.21 = ((bf16[1,32,5,3584]{3,2,0,1:T(8,128)(2,1)}), bf16[1,32,5,3584]{3,2,0,1:T(8,128)(2,1)}, u32[]{:S(2)}, u32[]{:S(2)}) async-start(bf16[1,32,5,3584]{3,2,0,1:T(8,128)(2,1)} %bitcast.1336), calls=%async_computation.21 | async-start | bytes 3670016 | tf_op jit(solution)/shard_map/all_to_all | solution.py:151
  1104.5 7.2 collective-permute-start.9
  1122.2 32.6 %all-to-all-start.22 = ((bf16[1,32,5,3584]{3,2,0,1:T(8,128)(2,1)}), bf16[1,32,5,3584]{3,2,0,1:T(8,128)(2,1)}, u32[]{:S(2)}, u32[]{:S(2)}) async-start(bf16[1,32,5,3584]{3,2,0,1:T(8,128)(2,1)} %bitcast.1328), calls=%async_computation.22 | async-start | bytes 3670016 | tf_op jit(solution)/shard_map/all_to_all | solution.py:144
  1168.2 31.8 %all-to-all-start.23 = ((bf16[1,32,5,3584]{3,2,0,1:T(8,128)(2,1)}), bf16[1,32,5,3584]{3,2,0,1:T(8,128)(2,1)}, u32[]{:S(2)}, u32[]{:S(2)}) async-start(bf16[1,32,5,3584]{3,2,0,1:T(8,128)(2,1)} %bitcast.1337), calls=%async_computation.23 | async-start | bytes 3670016 | tf_op jit(solution)/shard_map/all_to_all | solution.py:151
  1208.7 7.2 collective-permute-start.10
  1225.9 32.6 %all-to-all-start.24 = ((bf16[1,32,5,3584]{3,2,0,1:T(8,128)(2,1)}), bf16[1,32,5,3584]{3,2,0,1:T(8,128)(2,1)}, u32[]{:S(2)}, u32[]{:S(2)}) async-start(bf16[1,32,5,3584]{3,2,0,1:T(8,128)(2,1)} %bitcast.1349), calls=%async_computation.24 | async-start | bytes 3670016 | tf_op jit(solution)/shard_map/all_to_all | solution.py:144
  1271.9 31.9 %all-to-all-start.25 = ((bf16[1,32,5,3584]{3,2,0,1:T(8,128)(2,1)}), bf16[1,32,5,3584]{3,2,0,1:T(8,128)(2,1)}, u32[]{:S(2)}, u32[]{:S(2)}) async-start(bf16[1,32,5,3584]{3,2,0,1:T(8,128)(2,1)} %bitcast.1338), calls=%async_computation.25 | async-start | bytes 3670016 | tf_op jit(solution)/shard_map/all_to_all | solution.py:151
  1312.5 7.1 collective-permute-start.11
  1329.7 32.5 %all-to-all-start.26 = ((bf16[1,32,5,3584]{3,2,0,1:T(8,128)(2,1)}), bf16[1,32,5,3584]{3,2,0,1:T(8,128)(2,1)}, u32[]{:S(2)}, u32[]{:S(2)}) async-start(bf16[1,32,5,3584]{3,2,0,1:T(8,128)(2,1)} %bitcast.1340), calls=%async_computation.26 | async-start | bytes 3670016 | tf_op jit(solution)/shard_map/all_to_all | solution.py:144
  1373.5 31.1 %all-to-all-start.27 = ((bf16[1,32,5,3584]{3,2,0,1:T(8,128)(2,1)}), bf16[1,32,5,3584]{3,2,0,1:T(8,128)(2,1)S(1)}, u32[]{:S(2)}, u32[]{:S(2)}) async-start(bf16[1,32,5,3584]{3,2,0,1:T(8,128)(2,1)} %bitcast.261), calls=%async_computation.27 | async-start | bytes 3670016 | tf_op jit(solution)/shard_map/all_to_all | solution.py:151
  (150 other events, 619.0 us)
where the time goes:
time: 1430 us; the launch traced here: 1410 us
  waiting for transfers between devices  654 us (46%)
  local copies, waits for them, and re-layouts  245 us (17%)
  starting transfers between devices  232 us (16%)
  matrix products  158 us (11%)
  other arithmetic  117 us (8%)
    all_to_all x14, waiting for transfers between devices, dispatch_rows(): lax.all_to_all(for_sending(doubled), 'expert', split_axis=1, concat_axis=...  308 us
    all_to_all x14, waiting for transfers between devices, combine_rows(): lax.all_to_all(partial_value, 'expert', split_axis=1, concat_axis=1, tile...  301 us
    all_to_all x14, starting transfers between devices, dispatch_rows(): lax.all_to_all(for_sending(doubled), 'expert', split_axis=1, concat_axis=...  108 us
    all_to_all x14, starting transfers between devices, combine_rows(): lax.all_to_all(partial_value, 'expert', split_axis=1, concat_axis=1, tile...  93.2 us
    broadcast_in_dim x28, local copies, waits for them, and re-layouts, dispatch_rows(): jnp.broadcast_to(send_rows[:, :, None], (item_count, experts_here, 2, cap...  60.1 us
    dot_general x28, matrix products, times_transposed(): lax.dot_general(left_side, right_side, (((1,), (1,)), ((), ())), preferre...  54.6 us
    dynamic_slice x48, local copies, waits for them, and re-layouts, pick_micro(): return lax.dynamic_index_in_dim(stacked, position, 0, keepdims=False)  46.7 us
    dynamic_update_slice x48, other arithmetic, store_micro(): lax.dynamic_update_index_in_dim(stacked, jnp.where(enabled, values, previ...  44.9 us
  transfers between devices with their start and end apart: 40, of which 40 were waited for; matrix products, arithmetic and copies ran while one was open for 7% of the time, Pallas kernels for 0%

commit v1 on v0

v1 whole, which is shorter than its diff:
```python
import functools
import math

import jax
import jax.numpy as jnp
from jax import lax
from jax.experimental import pallas as pl
from jax.experimental.pallas import tpu as pltpu
from jax.sharding import PartitionSpec as P

EPSILON = 1e-06
PIECES = 4
MESH = pl.DeviceIdType.MESH


def grid_of(chips):
    rows = math.isqrt(chips)
    while chips % rows:
        rows -= 1
    return rows, chips // rows


def block_rows(capacity):
    return -(-PIECES * capacity // 8) * 8


def matmul(left, right):
    return jnp.dot(left, right, preferred_element_type=jnp.float32)


def matmul_t(left, right):
    return lax.dot_general(
        left, right, (((1,), (1,)), ((), ())), preferred_element_type=jnp.float32
    )


def relay_kernel(
    geometry,
    inputs_ref,
    cotangent_ref,
    gain_ref,
    router_ref,
    wg_hbm,
    wu_hbm,
    wd_hbm,
    row_table_ref,
    col_table_ref,
    ids_ref,
    out_ref,
    grad_ref,
    wg,
    wu,
    wd,
    acts,
    grads,
    unpack,
    repack,
    dispatch_send,
    dispatch_recv,
    partner_rows,
    combine_send,
    combine_recv,
    half_send,
    half_own,
    half_recv,
    rows_in,
    gate_saved,
    up_saved,
    picked,
    stats,
    weight_sem,
    act_sem,
    grad_sem,
    pipe_sem,
    dispatch_send_sem,
    dispatch_recv_sem,
    swap_send_sem,
    swap_recv_sem,
    half_send_sem,
    half_recv_sem,
    combine_send_sem,
    combine_recv_sem,
):
    sections, micro_count, chips, capacity, offsets, slots = geometry
    lines, columns = grid_of(chips)
    block = block_rows(capacity)
    tokens, width = acts.shape[1], acts.shape[2]
    piece = width // PIECES
    group = chips * capacity
    hidden = wg.shape[1]
    experts = router_ref.shape[1]
    section = lax.axis_index("pipe")
    place = lax.axis_index("expert")
    core = lax.rem(place, 2)
    chip = place // 2
    line, column = chip // columns, lax.rem(chip, columns)
    partner = chip * 2 + (1 - core)
    others = pl.ds(1, chips - 1)

    def peer(step, sign):
        to_line = lax.rem(line + sign * (step // columns) + lines, lines)
        to_column = lax.rem(column + sign * lax.rem(step, columns) + columns, columns)
        return {"expert": (to_line * columns + to_column) * 2 + core}

    def pieces_of(value):
        return [value[:, q * piece : (q + 1) * piece] for q in range(PIECES)]

    barrier = pltpu.get_barrier_semaphore()

    def greet(step, carry):
        pl.semaphore_signal(barrier, inc=1, device_id=peer(step, 1), device_id_type=MESH)
        return carry

    weights = [
        pltpu.make_async_copy(source, target, weight_sem.at[i])
        for i, (source, target) in enumerate([(wg_hbm, wg), (wu_hbm, wu), (wd_hbm, wd)])
    ]

    @pl.when(section == 0)
    def _():
        for m in range(micro_count):
            pltpu.make_async_copy(inputs_ref.at[m], acts.at[m], act_sem.at[m]).start()

    @pl.when(section == sections - 1)
    def _():
        for m in range(micro_count):
            pltpu.make_async_copy(cotangent_ref.at[m], grads.at[m], grad_sem.at[m]).start()

    for copy in weights:
        copy.start()
    lax.fori_loop(1, chips, greet, 0)
    pl.semaphore_signal(barrier, inc=1, device_id={"expert": partner}, device_id_type=MESH)
    for sign in (1, sections - 1):
        pl.semaphore_signal(
            barrier,
            inc=1,
            device_id={"pipe": lax.rem(section + sign, sections)},
            device_id_type=MESH,
        )

    def place_of(number):
        within = lax.rem(number, block)
        q = within // capacity
        row = q * group + (number // block) * capacity + lax.rem(within, capacity)
        return jnp.where(within < PIECES * capacity, row, -1)

    wide = lax.broadcasted_iota(jnp.int32, (PIECES * group, chips * block), 1)
    tall = lax.broadcasted_iota(jnp.int32, (PIECES * group, chips * block), 0)
    unpack[...] = jnp.where(place_of(wide) == tall, 1.0, 0.0).astype(jnp.bfloat16)
    tall = lax.broadcasted_iota(jnp.int32, (chips * block, PIECES * group), 0)
    wide = lax.broadcasted_iota(jnp.int32, (chips * block, PIECES * group), 1)
    repack[...] = jnp.where(place_of(tall) == wide, 1.0, 0.0).astype(jnp.bfloat16)

    pl.semaphore_wait(barrier, chips - 1 + 1 + 2)

    def wait_all(buffer, semaphore):
        pltpu.make_async_copy(buffer, buffer, semaphore).wait()

    def send_blocks(send, recv, send_sem, recv_sem, sign):
        def start(step, carry):
            pltpu.make_async_remote_copy(
                src_ref=send.at[step],
                dst_ref=recv.at[step],
                send_sem=send_sem,
                recv_sem=recv_sem,
                device_id=peer(step, sign),
                device_id_type=MESH,
            ).start()
            return carry

        lax.fori_loop(1, chips, start, 0)

    def post(values, send, recv, send_sem, recv_sem, sign):
        values = values.astype(jnp.bfloat16).reshape(chips, block, piece)
        recv[0] = values[0]
        send[others] = values[1:]
        send_blocks(send, recv, send_sem, recv_sem, sign)

    def table_rows(m):
        lanes = PIECES * tokens
        rows = lax.broadcasted_iota(jnp.int32, (chips * block, 2 * lanes), 0)
        return jnp.where(rows == row_table_ref[m], 1.0, 0.0).astype(jnp.bfloat16)

    def table_columns(m):
        places = lax.broadcasted_iota(jnp.int32, (2 * PIECES * tokens, chips * block), 1)
        return jnp.where(places == col_table_ref[m], 1.0, 0.0).astype(jnp.bfloat16)

    def expert_hot(m, k):
        names = lax.broadcasted_iota(jnp.int32, (tokens, experts), 1)
        return jnp.where(names == ids_ref[m, k], 1.0, 0.0)

    def swap_and_unpack(m, way):
        slot = 2 * way + lax.rem(m, 2)
        wait_all(dispatch_recv.at[m, others], dispatch_recv_sem.at[m])
        swap = pltpu.make_async_remote_copy(
            src_ref=dispatch_recv.at[m],
            dst_ref=partner_rows.at[m],
            send_sem=swap_send_sem,
            recv_sem=swap_recv_sem.at[m],
            device_id={"expert": partner},
            device_id_type=MESH,
        )
        swap.start()
        wait_all(dispatch_send.at[slot, others], dispatch_send_sem.at[slot])
        for part, source in enumerate((dispatch_recv, partner_rows)):
            if part == 1:
                swap.wait()
            flat = source[m].reshape(chips * block, piece)
            rows = matmul(unpack[...], flat).astype(jnp.bfloat16)
            for q in range(PIECES):
                rows_in[q, part * group : (part + 1) * group] = rows[q * group : (q + 1) * group]

    def halves_and_combine(m, way, product):
        slot = 2 * way + lax.rem(m, 2)

        def half_copy(q):
            return pltpu.make_async_remote_copy(
                src_ref=half_send.at[q],
                dst_ref=half_recv.at[m, q],
                send_sem=half_send_sem,
                recv_sem=half_recv_sem.at[m],
                device_id={"expert": partner},
                device_id_type=MESH,
            )

        for q in range(PIECES):
            part = product(q).astype(jnp.bfloat16)
            half_own[q] = part[:group]
            half_send[q] = part[group:]
            half_copy(q).start()
        wait_all(half_recv.at[m], half_recv_sem.at[m])
        total = half_own[...].astype(jnp.float32) + half_recv[m].astype(jnp.float32)
        total = total.astype(jnp.bfloat16).reshape(PIECES * group, piece)
        post(
            matmul(repack[...], total),
            combine_send.at[slot],
            combine_recv.at[m],
            combine_send_sem.at[slot],
            combine_recv_sem.at[m],
            -1,
        )
        wait_all(half_send, half_send_sem)

    def forward_send(m):
        wait_all(acts.at[m], act_sem.at[m])
        wide_in = acts[m].astype(jnp.float32)
        scale = lax.rsqrt(jnp.mean(wide_in * wide_in, axis=1, keepdims=True) + EPSILON)
        normed = (wide_in * scale * gain_ref[...]).astype(jnp.bfloat16)
        stacked = jnp.concatenate(pieces_of(normed), axis=0)
        table = table_rows(m)
        lanes = PIECES * tokens
        slot = lax.rem(m, 2)
        post(
            matmul(table[:, :lanes] + table[:, lanes:], stacked),
            dispatch_send.at[slot],
            dispatch_recv.at[m],
            dispatch_send_sem.at[slot],
            dispatch_recv_sem.at[m],
            1,
        )
        logits = matmul(normed, router_ref[...])
        chances = []
        for k in range(2):
            score = jnp.sum(logits * expert_hot(m, k), axis=1, keepdims=True)
            chances.append(1.0 / (1.0 + jnp.exp(-score)))
        total = chances[0] + chances[1]
        stats[m, 0] = scale
        stats[m, 1] = chances[0]
        stats[m, 2] = chances[1]
        stats[m, 3] = chances[0] / total
        stats[m, 4] = chances[1] / total

    def forward_expert(m):
        swap_and_unpack(m, 0)
        gate_pre = jnp.zeros((2 * group, hidden), jnp.float32)
        up_pre = jnp.zeros((2 * group, hidden), jnp.float32)
        for q in range(PIECES):
            span = slice(q * piece, (q + 1) * piece)
            gate_pre += matmul(rows_in[q], wg[span])
            up_pre += matmul(rows_in[q], wu[span])
        gate_saved[m] = gate_pre
        up_saved[m] = up_pre
        inner = (gate_pre / (1.0 + jnp.exp(-gate_pre)) * up_pre).astype(jnp.bfloat16)
        halves_and_combine(
            m, 0, lambda q: matmul(inner, wd[:, q * piece : (q + 1) * piece])
        )

    def forward_finish(m):
        wait_all(combine_recv.at[m, others], combine_recv_sem.at[m])
        slot = lax.rem(m, 2)
        wait_all(combine_send.at[slot, others], combine_send_sem.at[slot])
        found = matmul(table_columns(m), combine_recv[m].reshape(chips * block, piece))
        for q in range(PIECES):
            span = slice(q * piece, (q + 1) * piece)
            total = acts[m, :, span].astype(jnp.float32)
            for k in range(2):
                begin = (k * PIECES + q) * tokens
                rows = found[begin : begin + tokens]
                picked[m, k, :, span] = rows.astype(jnp.bfloat16)
                total += stats[m, 3 + k] * rows
            out_ref[m, :, span] = total.astype(jnp.bfloat16)

        @pl.when(section < sections - 1)
        def _():
            pltpu.make_async_remote_copy(
                src_ref=out_ref.at[m],
                dst_ref=acts.at[m],
                send_sem=pipe_sem.at[0],
                recv_sem=act_sem.at[m],
                device_id={"pipe": section + 1},
                device_id_type=MESH,
            ).start()

    def backward_send(m):
        wait_all(grads.at[m], grad_sem.at[m])
        upstream = grads[m].astype(jnp.float32)
        stacked = []
        for k in range(2):
            stacked += pieces_of((stats[m, 3 + k] * upstream).astype(jnp.bfloat16))
        slot = 2 + lax.rem(m, 2)
        post(
            matmul(table_rows(m), jnp.concatenate(stacked, axis=0)),
            dispatch_send.at[slot],
            dispatch_recv.at[m],
            dispatch_send_sem.at[slot],
            dispatch_recv_sem.at[m],
            1,
        )
        slopes = [
            jnp.sum(upstream * picked[m, k].astype(jnp.float32), axis=1, keepdims=True)
            for k in range(2)
        ]
        weighted = stats[m, 3] * slopes[0] + stats[m, 4] * slopes[1]
        total = stats[m, 1] + stats[m, 2]
        for k in range(2):
            chance = stats[m, 1 + k]
            stats[m, 5 + k] = (slopes[k] - weighted) / total * chance * (1.0 - chance)

    def backward_expert(m):
        swap_and_unpack(m, 1)
        hidden_grad = jnp.zeros((2 * group, hidden), jnp.float32)
        for q in range(PIECES):
            hidden_grad += matmul_t(rows_in[q], wd[:, q * piece : (q + 1) * piece])
        gate_pre = gate_saved[m]
        sigmoid = 1.0 / (1.0 + jnp.exp(-gate_pre))
        pre_grad = (
            hidden_grad * up_saved[m] * sigmoid * (1.0 + gate_pre * (1.0 - sigmoid))
        ).astype(jnp.bfloat16)
        up_grad = (hidden_grad * gate_pre * sigmoid).astype(jnp.bfloat16)

        def product(q):
            span = slice(q * piece, (q + 1) * piece)
            return matmul_t(pre_grad, wg[span]) + matmul_t(up_grad, wu[span])

        halves_and_combine(m, 1, product)

    def backward_finish(m):
        wait_all(combine_recv.at[m, others], combine_recv_sem.at[m])
        slot = 2 + lax.rem(m, 2)
        wait_all(combine_send.at[slot, others], combine_send_sem.at[slot])
        table = table_columns(m)
        lanes = PIECES * tokens
        summed = matmul(
            table[:lanes] + table[lanes:], combine_recv[m].reshape(chips * block, piece)
        )
        router_table = (
            stats[m, 5] * expert_hot(m, 0) + stats[m, 6] * expert_hot(m, 1)
        ).astype(jnp.bfloat16)
        scale = stats[m, 0]
        inner = jnp.zeros((tokens, 1), jnp.float32)
        kept = []
        for q in range(PIECES):
            span = slice(q * piece, (q + 1) * piece)
            routed = matmul_t(router_table, router_ref[span])
            normed_grad = (summed[q * tokens : (q + 1) * tokens] + routed) * gain_ref[:, span]
            inner += jnp.sum(
                acts[m, :, span].astype(jnp.float32) * normed_grad, axis=1, keepdims=True
            )
            kept.append(normed_grad)
        inner = scale * scale * scale * (inner / width)
        for q in range(PIECES):
            span = slice(q * piece, (q + 1) * piece)
            result = grads[m, :, span].astype(jnp.float32) + scale * kept[q]
            result -= acts[m, :, span].astype(jnp.float32) * inner
            grad_ref[m, :, span] = result.astype(jnp.bfloat16)

        @pl.when(section > 0)
        def _():
            pltpu.make_async_remote_copy(
                src_ref=grad_ref.at[m],
                dst_ref=grads.at[m],
                send_sem=pipe_sem.at[1],
                recv_sem=grad_sem.at[m],
                device_id={"pipe": section - 1},
                device_id_type=MESH,
            ).start()

    to_expert, to_finish, stage = offsets
    turn = sections * stage
    forward_at = section * stage
    backward_at = turn + (sections - 1 - section) * stage
    steps = {
        "FA": (forward_send, forward_at),
        "FB": (forward_expert, forward_at + to_expert),
        "FC": (forward_finish, forward_at + to_finish),
        "BA": (backward_send, backward_at),
        "BB": (backward_expert, backward_at + to_expert),
        "BC": (backward_finish, backward_at + to_finish),
    }

    for copy in weights:
        copy.wait()

    def slot_body(i, carry):
        for name in slots:
            step, begin = steps[name]
            m = i - begin

            @pl.when((m >= 0) & (m < micro_count))
            def _():
                step(m)

        return carry

    last = turn + (sections - 1) * stage + to_finish + micro_count
    lax.fori_loop(0, last, slot_body, 0)

    @pl.when(section < sections - 1)
    def _():
        wait_all(out_ref, pipe_sem.at[0])

    @pl.when(section > 0)
    def _():
        wait_all(grad_ref, pipe_sem.at[1])


def routing_tables(ids, chips, capacity):
    lines, columns = grid_of(chips)
    micro_count, tokens, top_count = ids.shape
    chip = lax.axis_index("expert") // 2
    flat = ids.reshape(micro_count, tokens * top_count)
    number = jnp.arange(tokens * top_count)
    same = (flat[:, :, None] == flat[:, None, :]) & (number[None, None, :] < number[None, :, None])
    rank = jnp.sum(same.astype(jnp.int32), axis=2).reshape(ids.shape)
    to_line = (ids // columns - chip // columns + lines) % lines
    to_column = (ids % columns - chip % columns + columns) % columns
    place = (to_line * columns + to_column) * block_rows(capacity) + rank
    place = jnp.moveaxis(place, 2, 1)[:, :, None, :]
    place = place + (jnp.arange(PIECES, dtype=jnp.int32) * capacity)[None, None, :, None]
    flat_place = place.reshape(micro_count, top_count * PIECES * tokens)
    return flat_place[:, None, :], flat_place[:, :, None], jnp.moveaxis(ids, 2, 1)[..., None]


OFFSETS = (1, 3, 4)
SLOTS = ("FC", "BC", "FA", "BA", "FB", "BB")


def on_device(
    inputs, cotangent, norm_gain, router_weight, gate_weight, up_weight, down_weight, route_ids
):
    sections = lax.axis_size("pipe")
    chips = lax.axis_size("expert") // 2
    micro_count, tokens, width = inputs.shape
    experts = router_weight.shape[2]
    top_count = route_ids.shape[3]
    capacity = min(tokens, (5 * tokens * top_count + 4 * experts - 1) // (4 * experts))
    hidden = gate_weight.shape[2]
    block = block_rows(capacity)
    piece = width // PIECES
    group = chips * capacity
    tables = routing_tables(route_ids[0], chips, capacity)
    anywhere = pl.BlockSpec(memory_space=pl.ANY)
    inside = pl.BlockSpec(memory_space=pltpu.VMEM)
    bf16, f32 = jnp.bfloat16, jnp.float32
    out = jax.ShapeDtypeStruct((micro_count, tokens, width), bf16)
    dma = pltpu.SemaphoreType.DMA
    geometry = (sections, micro_count, chips, capacity, OFFSETS, SLOTS)
    forward_out, backward_out = pl.pallas_call(
        functools.partial(relay_kernel, geometry),
        out_shape=(out, out),
        in_specs=[anywhere] * 2 + [inside] * 2 + [anywhere] * 3 + [inside] * 3,
        out_specs=(inside, inside),
        scratch_shapes=[
            pltpu.VMEM((width, hidden), bf16),
            pltpu.VMEM((width, hidden), bf16),
            pltpu.VMEM((hidden, width), bf16),
            pltpu.VMEM((micro_count, tokens, width), bf16),
            pltpu.VMEM((micro_count, tokens, width), bf16),
            pltpu.VMEM((PIECES * group, chips * block), bf16),
            pltpu.VMEM((chips * block, PIECES * group), bf16),
            pltpu.VMEM((4, chips, block, piece), bf16),
            pltpu.VMEM((micro_count, chips, block, piece), bf16),
            pltpu.VMEM((micro_count, chips, block, piece), bf16),
            pltpu.VMEM((4, chips, block, piece), bf16),
            pltpu.VMEM((micro_count, chips, block, piece), bf16),
            pltpu.VMEM((PIECES, group, piece), bf16),
            pltpu.VMEM((PIECES, group, piece), bf16),
            pltpu.VMEM((micro_count, PIECES, group, piece), bf16),
            pltpu.VMEM((PIECES, 2 * group, piece), bf16),
            pltpu.VMEM((micro_count, 2 * group, hidden), f32),
            pltpu.VMEM((micro_count, 2 * group, hidden), f32),
            pltpu.VMEM((micro_count, top_count, tokens, width), bf16),
            pltpu.VMEM((micro_count, 7, tokens, 1), f32),
            dma((3,)),
            dma((micro_count,)),
            dma((micro_count,)),
            dma((2,)),
            dma((4,)),
            dma((micro_count,)),
            dma,
            dma((micro_count,)),
            dma,
            dma((micro_count,)),
            dma((4,)),
            dma((micro_count,)),
        ],
        compiler_params=pltpu.CompilerParams(
            collective_id=0, has_side_effects=True, vmem_limit_bytes=66_000_000
        ),
    )(
        inputs,
        cotangent,
        norm_gain,
        router_weight[0],
        gate_weight[0],
        up_weight[0],
        down_weight[0],
        *tables,
    )
    return (forward_out[None], backward_out[None])


def solution(mesh):
    return jax.shard_map(
        on_device,
        mesh=mesh,
        in_specs=(
            P(None, "expert", None),
            P(None, "expert", None),
            P("pipe", None),
            P("pipe", None, None),
            P("pipe", None, "expert"),
            P("pipe", None, "expert"),
            P("pipe", "expert", None),
            P("pipe", None, "expert", None),
        ),
        out_specs=(P("pipe", None, "expert", None), P("pipe", None, "expert", None)),
        check_vma=False,
    )
```

time: 1430 us -> 434 us (0.30); the launches traced: 1410 us -> 433 us
  waiting for transfers between devices: 654 us -> 0 us
  Pallas kernels: 0 us -> 421 us
  local copies, waits for them, and re-layouts: 245 us -> 9.73 us
  starting transfers between devices: 232 us -> 0 us
  matrix products: 158 us -> 0 us
  other arithmetic: 117 us -> 2 us
    all_to_all x28 -> x0, waiting for transfers between devices: 609 us -> none  [the longest x14 308 us: dispatch_rows(): lax.all_to_all(for_sending(doubled), 'expert', split_axis=1, concat_axis=...]
    pallas_call x0 -> x1, Pallas kernels: none -> 421 us  [on_device(): pl.pallas_call(functools.partial(relay_kernel, geometry), out_shape=(out,...]
    all_to_all x28 -> x0, starting transfers between devices: 201 us -> none  [the longest x14 108 us: dispatch_rows(): lax.all_to_all(for_sending(doubled), 'expert', split_axis=1, concat_axis=...]
    dot_general x91 -> x0, matrix products: 158 us -> none  [the longest x28 54.6 us: times_transposed(): lax.dot_general(left_side, right_side, (((1,), (1,)), ((), ())), preferre...]
    broadcast_in_dim x32 -> x1, local copies, waits for them, and re-layouts: 63.2 us -> 1.45 us  [routing_tables(): jnp.moveaxis(ids, 2, 1)[..., None]]
    convert_element_type x50 -> x0, other arithmetic: 50 us -> none  [the longest x14 25.6 us: combine_rows(): returned.reshape(item_count, group_size // 2, 2, capacity, model_width)]
    dynamic_slice x48 -> x0, local copies, waits for them, and re-layouts: 46.7 us -> none  [pick_micro(): return lax.dynamic_index_in_dim(stacked, position, 0, keepdims=False)]
    dynamic_update_slice x48 -> x0, other arithmetic: 44.9 us -> none  [store_micro(): lax.dynamic_update_index_in_dim(stacked, jnp.where(enabled, values, previ...]
  transfers between devices with their start and end apart: 40 -> 0, of which waited for: 40 -> 0; matrix products, arithmetic and copies ran while one was open for 7% -> 0% of each run, Pallas kernels for 0% -> 0%
where the time goes in v1:
time: 434 us; the launch traced here: 433 us
  Pallas kernels  421 us (97%)
  local copies, waits for them, and re-layouts  9.73 us (2%)
    pallas_call x1, Pallas kernels, on_device(): pl.pallas_call(functools.partial(relay_kernel, geometry), out_shape=(out,...  421 us

profile of v1, /device:TPU:1, one launch (start us, length us, event | category | flops | bytes accessed | tf_op | source)
XLA Modules:
  0.0 433.3 jit_solution(1978642909841410007)
XLA Ops:
  0.7 0.1 add.86
  0.8 0.1 add.87
  0.8 0.8 copy.31
  1.6 0.1 copy.33
  1.7 0.2 convert_reduce_fusion
  1.9 0.1 copy.35
  2.0 0.3 add_bitcast_fusion
  2.3 0.1 copy.36
  2.4 0.1 add.85
  2.5 0.6 broadcast_add_fusion.1.row_table_ref
  3.1 1.4 copy.40.ids_ref
  4.5 0.5 add.93
  5.1 0.9 broadcast_add_fusion.col_table_ref
  6.0 2.1 copy.30
  8.1 420.8 %shard_map.95 = (bf16[4,32,3584]{2,1,0:T(8,128)(2,1)}, bf16[4,32,3584]{2,1,0:T(8,128)(2,1)}) custom-call(bf16[4,32,3584]{2,1,0:T(8,128)(2,1)} %inputs_ref.1, bf16[4,32,3584]{2,1,0:T(8,128)(2,1)} %cotangent_ref.1, f32[1,3584]{1,0:T(1,128)} %gain_ref.1, bf16[3584,16]{1,0:T(8,128)(2,1)} %bitcast.28, bf16[3584,512]{1,0:T(8,128)(2,1)} %bitcast.29, ...), custom_call_target="tpu_custom_call" | custom-call | tf_op jit(solution)/shard_map/pallas_call | solution.py:478
  429.0 2.2 copy.44
  431.1 2.2 copy.45
  (3 shorter events, 0.0 us)

commit v2 on v1

v2 whole, which is shorter than its diff:
```python
import functools
import math

import jax
import jax.numpy as jnp
from jax import lax
from jax.experimental import pallas as pl
from jax.experimental.pallas import tpu as pltpu
from jax.sharding import PartitionSpec as P

EPSILON = 1e-06
PIECES = 7
CHUNKS = 2
MESH = pl.DeviceIdType.MESH


def grid_of(chips):
    rows = math.isqrt(chips)
    while chips % rows:
        rows -= 1
    return rows, chips // rows


def block_rows(capacity):
    return -(-PIECES * capacity // 8) * 8


def matmul(left, right):
    return jnp.dot(left, right, preferred_element_type=jnp.float32)


def matmul_t(left, right):
    return lax.dot_general(
        left, right, (((1,), (1,)), ((), ())), preferred_element_type=jnp.float32
    )


def relay_kernel(
    geometry,
    inputs_ref,
    cotangent_ref,
    gain_ref,
    router_ref,
    wg_hbm,
    wu_hbm,
    wd_hbm,
    row_table_ref,
    col_table_ref,
    ids_ref,
    out_ref,
    grad_ref,
    wg,
    wu,
    wd,
    acts,
    grads,
    unpack,
    repack,
    dispatch_send,
    dispatch_recv,
    partner_rows,
    combine_send,
    combine_recv,
    half_send,
    half_own,
    half_recv,
    rows_in,
    squares,
    gate_saved,
    up_saved,
    hidden_grad,
    picked,
    kept,
    stats,
    weight_sem,
    act_sem,
    grad_sem,
    pipe_sem,
    dispatch_send_sem,
    dispatch_recv_sem,
    swap_send_sem,
    swap_recv_sem,
    half_send_sem,
    half_recv_sem,
    combine_send_sem,
    combine_recv_sem,
):
    sections, micro_count, chips, capacity = geometry
    lines, columns = grid_of(chips)
    block = block_rows(capacity)
    tokens, part_width = acts.shape[2], acts.shape[3]
    width = CHUNKS * part_width
    piece = part_width // PIECES
    group = chips * capacity
    hidden = wg.shape[1]
    experts = router_ref.shape[1]
    lanes = PIECES * tokens
    section = lax.axis_index("pipe")
    place = lax.axis_index("expert")
    core = lax.rem(place, 2)
    chip = place // 2
    line, column = chip // columns, lax.rem(chip, columns)
    partner = chip * 2 + (1 - core)
    others = pl.ds(1, chips - 1)

    def peer(step, sign):
        to_line = lax.rem(line + sign * (step // columns) + lines, lines)
        to_column = lax.rem(column + sign * lax.rem(step, columns) + columns, columns)
        return {"expert": (to_line * columns + to_column) * 2 + core}

    def span(c):
        return slice(c * part_width, (c + 1) * part_width)

    def pieces_of(value):
        return [value[:, q * piece : (q + 1) * piece] for q in range(PIECES)]

    barrier = pltpu.get_barrier_semaphore()

    def greet(step, carry):
        pl.semaphore_signal(barrier, inc=1, device_id=peer(step, 1), device_id_type=MESH)
        return carry

    weights = [
        pltpu.make_async_copy(source, target, weight_sem.at[i])
        for i, (source, target) in enumerate([(wg_hbm, wg), (wu_hbm, wu), (wd_hbm, wd)])
    ]

    def fetch(source, target, semaphore):
        for m in range(micro_count):
            for c in range(CHUNKS):
                pltpu.make_async_copy(
                    source.at[m, :, span(c)], target.at[m, c], semaphore.at[m * CHUNKS + c]
                ).start()

    @pl.when(section == 0)
    def _():
        fetch(inputs_ref, acts, act_sem)

    @pl.when(section == sections - 1)
    def _():
        fetch(cotangent_ref, grads, grad_sem)

    for copy in weights:
        copy.start()
    lax.fori_loop(1, chips, greet, 0)
    pl.semaphore_signal(barrier, inc=1, device_id={"expert": partner}, device_id_type=MESH)
    for sign in (1, sections - 1):
        pl.semaphore_signal(
            barrier,
            inc=1,
            device_id={"pipe": lax.rem(section + sign, sections)},
            device_id_type=MESH,
        )

    def place_of(number):
        within = lax.rem(number, block)
        q = within // capacity
        row = q * group + (number // block) * capacity + lax.rem(within, capacity)
        return jnp.where(within < PIECES * capacity, row, -1)

    shape = (PIECES * group, chips * block)
    wide = place_of(lax.broadcasted_iota(jnp.int32, (1, shape[1]), 1))
    unpack[...] = jnp.where(
        lax.broadcasted_iota(jnp.int32, shape, 0) == wide, 1.0, 0.0
    ).astype(jnp.bfloat16)
    tall = place_of(lax.broadcasted_iota(jnp.int32, (shape[1], 1), 0))
    repack[...] = jnp.where(
        lax.broadcasted_iota(jnp.int32, shape[::-1], 1) == tall, 1.0, 0.0
    ).astype(jnp.bfloat16)

    pl.semaphore_wait(barrier, chips - 1 + 1 + 2)

    def wait_all(buffer, semaphore):
        pltpu.make_async_copy(buffer, buffer, semaphore).wait()

    def post(values, m, c, send, recv, send_sem, recv_sem, sign):
        values = values.astype(jnp.bfloat16).reshape(chips, block, piece)
        recv[m, c, 0] = values[0]
        send[m, c, others] = values[1:]

        def start(step, carry):
            pltpu.make_async_remote_copy(
                src_ref=send.at[m, c, step],
                dst_ref=recv.at[m, c, step],
                send_sem=send_sem.at[m * CHUNKS + c],
                recv_sem=recv_sem.at[m * CHUNKS + c],
                device_id=peer(step, sign),
                device_id_type=MESH,
            ).start()
            return carry

        lax.fori_loop(1, chips, start, 0)

    def dispatch(values, m, c):
        post(
            values, m, c, dispatch_send, dispatch_recv, dispatch_send_sem, dispatch_recv_sem, 1
        )

    def table_rows(m):
        rows = lax.broadcasted_iota(jnp.int32, (chips * block, 2 * lanes), 0)
        return jnp.where(rows == row_table_ref[m], 1.0, 0.0).astype(jnp.bfloat16)

    def table_columns(m):
        places = lax.broadcasted_iota(jnp.int32, (2 * lanes, chips * block), 1)
        return jnp.where(places == col_table_ref[m], 1.0, 0.0).astype(jnp.bfloat16)

    def expert_hot(m, k):
        names = lax.broadcasted_iota(jnp.int32, (tokens, experts), 1)
        return jnp.where(names == ids_ref[m, k], 1.0, 0.0)

    def take_rows(m, c, way):
        number = m * CHUNKS + c
        wait_all(dispatch_recv.at[m, c, others], dispatch_recv_sem.at[number])
        swap = pltpu.make_async_remote_copy(
            src_ref=dispatch_recv.at[m, c],
            dst_ref=partner_rows.at[m, c],
            send_sem=swap_send_sem,
            recv_sem=swap_recv_sem.at[number],
            device_id={"expert": partner},
            device_id_type=MESH,
        )
        swap.start()
        wait_all(dispatch_send.at[m, c, others], dispatch_send_sem.at[number])
        for part, source in enumerate((dispatch_recv, partner_rows)):
            if part == 1:
                swap.wait()
            rows = matmul(unpack[...], source[m, c].reshape(chips * block, piece))
            mine = slice(part * group, (part + 1) * group)
            square = jnp.zeros((group, piece), jnp.float32)
            for q in range(PIECES):
                at = slice(c * part_width + q * piece, c * part_width + (q + 1) * piece)
                found = rows[q * group : (q + 1) * group]
                if way == 0:
                    square += found * found
                    found = found * gain_ref[:, at]
                rows_in[way, mine, at] = found.astype(jnp.bfloat16)
            if way == 0:
                square = jnp.sum(square, axis=1, keepdims=True)
                squares[mine] = square if c == 0 else squares[mine] + square

    def halves_and_combine(m, product):
        copies = []
        for c in range(CHUNKS):
            part = product(c).astype(jnp.bfloat16)
            for q, values in enumerate(pieces_of(part)):
                half_own[c, q] = values[:group]
                half_send[c, q] = values[group:]
            copy = pltpu.make_async_remote_copy(
                src_ref=half_send.at[c],
                dst_ref=half_recv.at[m, c],
                send_sem=half_send_sem.at[c],
                recv_sem=half_recv_sem.at[m * CHUNKS + c],
                device_id={"expert": partner},
                device_id_type=MESH,
            )
            copy.start()
            copies.append(copy)
        for c in range(CHUNKS):
            copies[c].wait()
            total = half_own[c].astype(jnp.float32) + half_recv[m, c].astype(jnp.float32)
            total = total.astype(jnp.bfloat16).reshape(PIECES * group, piece)
            post(
                matmul(repack[...], total),
                m,
                c,
                combine_send,
                combine_recv,
                combine_send_sem,
                combine_recv_sem,
                -1,
            )

    def forward_send(m, c):
        wait_all(acts.at[m, c], act_sem.at[m * CHUNKS + c])
        table = table_rows(m)
        stacked = jnp.concatenate(pieces_of(acts[m, c]), axis=0)
        dispatch(matmul(table[:, :lanes] + table[:, lanes:], stacked), m, c)
        if c < CHUNKS - 1:
            return
        square = jnp.zeros((tokens, 1), jnp.float32)
        for d in range(CHUNKS):
            wide_in = acts[m, d].astype(jnp.float32)
            square += jnp.sum(wide_in * wide_in, axis=1, keepdims=True)
        scale = lax.rsqrt(square / width + EPSILON)
        logits = jnp.zeros((tokens, experts), jnp.float32)
        for d in range(CHUNKS):
            wide_in = acts[m, d].astype(jnp.float32)
            normed = (wide_in * scale * gain_ref[:, span(d)]).astype(jnp.bfloat16)
            logits += matmul(normed, router_ref[span(d)])
        chances = []
        for k in range(2):
            score = jnp.sum(logits * expert_hot(m, k), axis=1, keepdims=True)
            chances.append(1.0 / (1.0 + jnp.exp(-score)))
        total = chances[0] + chances[1]
        stats[m, 0] = scale
        stats[m, 1] = chances[0]
        stats[m, 2] = chances[1]
        stats[m, 3] = chances[0] / total
        stats[m, 4] = chances[1] / total

    def forward_expert(m, c):
        take_rows(m, c, 0)
        gate_pre = matmul(rows_in[0, :, span(c)], wg[span(c)])
        up_pre = matmul(rows_in[0, :, span(c)], wu[span(c)])
        if c > 0:
            gate_pre += gate_saved[m]
            up_pre += up_saved[m]
        if c < CHUNKS - 1:
            gate_saved[m] = gate_pre
            up_saved[m] = up_pre
            return
        scale = lax.rsqrt(squares[...] / width + EPSILON)
        gate_pre = gate_pre * scale
        up_pre = up_pre * scale
        gate_saved[m] = gate_pre
        up_saved[m] = up_pre
        inner = (gate_pre / (1.0 + jnp.exp(-gate_pre)) * up_pre).astype(jnp.bfloat16)
        halves_and_combine(m, lambda d: matmul(inner, wd[:, span(d)]))

    def receive_combined(m, c):
        number = m * CHUNKS + c
        wait_all(combine_recv.at[m, c, others], combine_recv_sem.at[number])
        wait_all(combine_send.at[m, c, others], combine_send_sem.at[number])
        return combine_recv[m, c].reshape(chips * block, piece)

    def forward_finish(m, c):
        found = matmul(table_columns(m), receive_combined(m, c))
        for q in range(PIECES):
            at = slice(q * piece, (q + 1) * piece)
            total = acts[m, c, :, at].astype(jnp.float32)
            for k in range(2):
                begin = (k * PIECES + q) * tokens
                rows = found[begin : begin + tokens]
                picked[m, c, k, :, at] = rows.astype(jnp.bfloat16)
                total += stats[m, 3 + k] * rows
            begin = c * part_width + q * piece
            out_ref[m, :, begin : begin + piece] = total.astype(jnp.bfloat16)

        @pl.when(section < sections - 1)
        def _():
            pltpu.make_async_remote_copy(
                src_ref=out_ref.at[m, :, span(c)],
                dst_ref=acts.at[m, c],
                send_sem=pipe_sem.at[0],
                recv_sem=act_sem.at[m * CHUNKS + c],
                device_id={"pipe": section + 1},
                device_id_type=MESH,
            ).start()

    def backward_send(m, c):
        wait_all(grads.at[m, c], grad_sem.at[m * CHUNKS + c])
        upstream = grads[m, c].astype(jnp.float32)
        stacked = []
        for k in range(2):
            stacked += pieces_of((stats[m, 3 + k] * upstream).astype(jnp.bfloat16))
        dispatch(matmul(table_rows(m), jnp.concatenate(stacked, axis=0)), m, c)
        slopes = []
        for k in range(2):
            values = picked[m, c, k].astype(jnp.float32)
            slope = jnp.sum(upstream * values, axis=1, keepdims=True)
            slopes.append(slope if c == 0 else slope + stats[m, 5 + k])
        if c == CHUNKS - 1:
            weighted = stats[m, 3] * slopes[0] + stats[m, 4] * slopes[1]
            total = stats[m, 1] + stats[m, 2]
            for k in range(2):
                chance = stats[m, 1 + k]
                slopes[k] = (slopes[k] - weighted) / total * chance * (1.0 - chance)
        for k in range(2):
            stats[m, 5 + k] = slopes[k]

    def backward_expert(m, c):
        take_rows(m, c, 1)
        inner_grad = matmul_t(rows_in[1, :, span(c)], wd[:, span(c)])
        if c > 0:
            inner_grad += hidden_grad[...]
        if c < CHUNKS - 1:
            hidden_grad[...] = inner_grad
            return
        gate_pre = gate_saved[m]
        sigmoid = 1.0 / (1.0 + jnp.exp(-gate_pre))
        pre_grad = (
            inner_grad * up_saved[m] * sigmoid * (1.0 + gate_pre * (1.0 - sigmoid))
        ).astype(jnp.bfloat16)
        up_grad = (inner_grad * gate_pre * sigmoid).astype(jnp.bfloat16)
        halves_and_combine(
            m, lambda d: matmul_t(pre_grad, wg[span(d)]) + matmul_t(up_grad, wu[span(d)])
        )

    def backward_finish(m, c):
        table = table_columns(m)
        summed = matmul(table[:lanes] + table[lanes:], receive_combined(m, c))
        router_table = (
            stats[m, 5] * expert_hot(m, 0) + stats[m, 6] * expert_hot(m, 1)
        ).astype(jnp.bfloat16)
        routed = matmul_t(router_table, router_ref[span(c)])
        inner = jnp.zeros((tokens, piece), jnp.float32)
        for q in range(PIECES):
            at = slice(q * piece, (q + 1) * piece)
            begin = c * part_width + q * piece
            normed_grad = summed[q * tokens : (q + 1) * tokens] + routed[:, at]
            normed_grad = normed_grad * gain_ref[:, begin : begin + piece]
            inner += acts[m, c, :, at].astype(jnp.float32) * normed_grad
            kept[c, :, at] = normed_grad
        inner = jnp.sum(inner, axis=1, keepdims=True)
        if c < CHUNKS - 1:
            stats[m, 7] = inner
            return
        scale = stats[m, 0]
        inner = scale * scale * scale * ((inner + stats[m, 7]) / width)
        for d in range(CHUNKS):
            result = grads[m, d].astype(jnp.float32) + scale * kept[d]
            result -= acts[m, d].astype(jnp.float32) * inner
            grad_ref[m, :, span(d)] = result.astype(jnp.bfloat16)

            @pl.when(section > 0)
            def _():
                pltpu.make_async_remote_copy(
                    src_ref=grad_ref.at[m, :, span(d)],
                    dst_ref=grads.at[m, d],
                    send_sem=pipe_sem.at[1],
                    recv_sem=grad_sem.at[m * CHUNKS + d],
                    device_id={"pipe": section - 1},
                    device_id_type=MESH,
                ).start()

    for copy in weights:
        copy.wait()
    steps = (
        forward_send,
        forward_expert,
        forward_finish,
        backward_send,
        backward_expert,
        backward_finish,
    )
    words = order_words(sections, micro_count)

    def run(i, counts):
        word = jnp.int32(0)
        for s, row in enumerate(words):
            for w, number in enumerate(row):
                word = jnp.where((section == s) & (i // DIGITS == w), number, word)
        word = lax.fori_loop(0, lax.rem(i, DIGITS), lambda j, rest: rest // 8, word)
        kind = lax.rem(word, 8)
        for number, step in enumerate(steps):
            m, c = counts[number] // CHUNKS, lax.rem(counts[number], CHUNKS)
            for d in range(CHUNKS):

                @pl.when((kind == number) & (c == d))
                def _():
                    step(m, d)

        return tuple(
            count + jnp.where(kind == number, 1, 0) for number, count in enumerate(counts)
        )

    total_steps = 6 * micro_count * CHUNKS
    lax.fori_loop(0, total_steps, run, (jnp.int32(0),) * 6)

    @pl.when(section < sections - 1)
    def _():
        wait_all(out_ref, pipe_sem.at[0])

    @pl.when(section > 0)
    def _():
        wait_all(grad_ref, pipe_sem.at[1])


KINDS = "abcABC"
DIGITS = 10
ORDERS = (
    "aaaabbbbcaacaaccbbbbccccAABBACACBBACACBBACACBBCC",
    "aaababbbccacacababbbccccAABBACACBBACACBBACACBBCC",
    "aaababbbccacacababbbccccAABBAACCBBAACCBBAACCBBCC",
    "aaababbbccAAcaacABABbbBBCaCaccAACCbbBBccAACCBBCC",
)


def order_words(sections, micro_count):
    orders = ORDERS
    if (sections, micro_count) != (4, 4):
        orders = ("aabbcc" * micro_count + "AABBCC" * micro_count,) * sections
    words = []
    for order in orders:
        row = []
        for begin in range(0, len(order), DIGITS):
            digits = [KINDS.index(kind) for kind in order[begin : begin + DIGITS]]
            row.append(sum(digit * 8**j for j, digit in enumerate(digits)))
        words.append(row)
    return words


def routing_tables(ids, chips, capacity):
    lines, columns = grid_of(chips)
    micro_count, tokens, top_count = ids.shape
    chip = lax.axis_index("expert") // 2
    flat = ids.reshape(micro_count, tokens * top_count)
    number = jnp.arange(tokens * top_count)
    same = (flat[:, :, None] == flat[:, None, :]) & (number[None, None, :] < number[None, :, None])
    rank = jnp.sum(same.astype(jnp.int32), axis=2).reshape(ids.shape)
    to_line = (ids // columns - chip // columns + lines) % lines
    to_column = (ids % columns - chip % columns + columns) % columns
    place = (to_line * columns + to_column) * block_rows(capacity) + rank
    place = jnp.moveaxis(place, 2, 1)[:, :, None, :]
    place = place + (jnp.arange(PIECES, dtype=jnp.int32) * capacity)[None, None, :, None]
    flat_place = place.reshape(micro_count, top_count * PIECES * tokens)
    return flat_place[:, None, :], flat_place[:, :, None], jnp.moveaxis(ids, 2, 1)[..., None]


def on_device(
    inputs, cotangent, norm_gain, router_weight, gate_weight, up_weight, down_weight, route_ids
):
    sections = lax.axis_size("pipe")
    chips = lax.axis_size("expert") // 2
    micro_count, tokens, width = inputs.shape
    experts = router_weight.shape[2]
    top_count = route_ids.shape[3]
    capacity = min(tokens, (5 * tokens * top_count + 4 * experts - 1) // (4 * experts))
    hidden = gate_weight.shape[2]
    block = block_rows(capacity)
    part_width = width // CHUNKS
    piece = part_width // PIECES
    group = chips * capacity
    tables = routing_tables(route_ids[0], chips, capacity)
    anywhere = pl.BlockSpec(memory_space=pl.ANY)
    inside = pl.BlockSpec(memory_space=pltpu.VMEM)
    bf16, f32 = jnp.bfloat16, jnp.float32
    out = jax.ShapeDtypeStruct((micro_count, tokens, width), bf16)
    dma = pltpu.SemaphoreType.DMA
    geometry = (sections, micro_count, chips, capacity)
    blocks = (micro_count, CHUNKS, chips, block, piece)
    halves = (CHUNKS, PIECES, group, piece)
    parts = micro_count * CHUNKS
    forward_out, backward_out = pl.pallas_call(
        functools.partial(relay_kernel, geometry),
        out_shape=(out, out),
        in_specs=[anywhere] * 2 + [inside] * 2 + [anywhere] * 3 + [inside] * 3,
        out_specs=(inside, inside),
        scratch_shapes=[
            pltpu.VMEM((width, hidden), bf16),
            pltpu.VMEM((width, hidden), bf16),
            pltpu.VMEM((hidden, width), bf16),
            pltpu.VMEM((micro_count, CHUNKS, tokens, part_width), bf16),
            pltpu.VMEM((micro_count, CHUNKS, tokens, part_width), bf16),
            pltpu.VMEM((PIECES * group, chips * block), bf16),
            pltpu.VMEM((chips * block, PIECES * group), bf16),
            pltpu.VMEM(blocks, bf16),
            pltpu.VMEM(blocks, bf16),
            pltpu.VMEM(blocks, bf16),
            pltpu.VMEM(blocks, bf16),
            pltpu.VMEM(blocks, bf16),
            pltpu.VMEM(halves, bf16),
            pltpu.VMEM(halves, bf16),
            pltpu.VMEM((micro_count, *halves), bf16),
            pltpu.VMEM((2, 2 * group, width), bf16),
            pltpu.VMEM((2 * group, 1), f32),
            pltpu.VMEM((micro_count, 2 * group, hidden), f32),
            pltpu.VMEM((micro_count, 2 * group, hidden), f32),
            pltpu.VMEM((2 * group, hidden), f32),
            pltpu.VMEM((micro_count, CHUNKS, top_count, tokens, part_width), bf16),
            pltpu.VMEM((CHUNKS, tokens, part_width), f32),
            pltpu.VMEM((micro_count, 8, tokens, 1), f32),
            dma((3,)),
            dma((parts,)),
            dma((parts,)),
            dma((2,)),
            dma((parts,)),
            dma((parts,)),
            dma,
            dma((parts,)),
            dma((CHUNKS,)),
            dma((parts,)),
            dma((parts,)),
            dma((parts,)),
        ],
        compiler_params=pltpu.CompilerParams(
            collective_id=0, has_side_effects=True, vmem_limit_bytes=66_000_000
        ),
    )(
        inputs,
        cotangent,
        norm_gain,
        router_weight[0],
        gate_weight[0],
        up_weight[0],
        down_weight[0],
        *tables,
    )
    return (forward_out[None], backward_out[None])


def solution(mesh):
    return jax.shard_map(
        on_device,
        mesh=mesh,
        in_specs=(
            P(None, "expert", None),
            P(None, "expert", None),
            P("pipe", None),
            P("pipe", None, None),
            P("pipe", None, "expert"),
            P("pipe", None, "expert"),
            P("pipe", "expert", None),
            P("pipe", None, "expert", None),
        ),
        out_specs=(P("pipe", None, "expert", None), P("pipe", None, "expert", None)),
        check_vma=False,
    )
```

time: 434 us -> 370 us (0.85)
  Pallas kernels: 421 us -> 357 us
    pallas_call x1, Pallas kernels: 421 us -> 357 us  [on_device(): pl.pallas_call(functools.partial(relay_kernel, geometry), out_shape=(out,...]
where the time goes in v2:
time: 370 us
  Pallas kernels  357 us (96%)
  local copies, waits for them, and re-layouts  10.1 us (3%)
    pallas_call x1, Pallas kernels, on_device(): pl.pallas_call(functools.partial(relay_kernel, geometry), out_shape=(out,...  357 us

profile of v2, /device:TPU:1, one launch (start us, length us, event | category | flops | bytes accessed | tf_op | source)
XLA Modules:
  0.0 370.0 jit_solution(11058795378801517671)
XLA Ops:
  0.7 0.1 add.86
  0.8 0.1 add.87
  0.8 0.8 copy.33
  1.6 0.1 copy.35
  1.7 0.2 convert_reduce_fusion
  1.9 0.1 copy.37
  2.0 0.3 add_bitcast_fusion
  2.3 0.1 copy.38
  2.4 0.1 add.93
  2.5 0.6 broadcast_add_fusion.1.row_table_ref
  3.1 1.4 copy.44.ids_ref
  4.5 0.9 add.94
  5.5 1.1 broadcast_add_fusion.col_table_ref
  6.5 2.1 copy.32
  8.7 357.0 %shard_map.95 = (bf16[4,32,3584]{2,1,0:T(8,128)(2,1)}, bf16[4,32,3584]{2,1,0:T(8,128)(2,1)}) custom-call(bf16[4,32,3584]{2,1,0:T(8,128)(2,1)} %inputs_ref.1, bf16[4,32,3584]{2,1,0:T(8,128)(2,1)} %cotangent_ref.1, f32[1,3584]{1,0:T(1,128)} %gain_ref.1, bf16[3584,16]{1,0:T(8,128)(2,1)} %bitcast.28, bf16[3584,512]{1,0:T(8,128)(2,1)} %bitcast.29, ...), custom_call_target="tpu_custom_call" | custom-call | tf_op jit(solution)/shard_map/pallas_call | solution.py:534
  365.6 2.2 copy.48
  367.8 2.2 copy.49
  (3 shorter events, 0.0 us)

commit v3 on v2

v3 whole, which is shorter than its diff:
```python
import functools
import math

import jax
import jax.numpy as jnp
from jax import lax
from jax.experimental import pallas as pl
from jax.experimental.pallas import tpu as pltpu
from jax.sharding import PartitionSpec as P

EPSILON = 1e-06
CHUNK_PIECES = (8, 6)
CHUNKS = len(CHUNK_PIECES)
MESH = pl.DeviceIdType.MESH


def grid_of(chips):
    rows = math.isqrt(chips)
    while chips % rows:
        rows -= 1
    return rows, chips // rows


def block_rows(c, capacity):
    return -(-CHUNK_PIECES[c] * capacity // 8) * 8


def matmul(left, right):
    return jnp.dot(left, right, preferred_element_type=jnp.float32)


def matmul_t(left, right):
    return lax.dot_general(
        left, right, (((1,), (1,)), ((), ())), preferred_element_type=jnp.float32
    )


def relay_kernel(
    geometry,
    inputs_ref,
    cotangent_ref,
    gain_ref,
    router_ref,
    wg_hbm,
    wu_hbm,
    wd_hbm,
    ids_ref,
    out_ref,
    grad_ref,
    wg,
    wu,
    wd,
    acts,
    grads,
    unpack,
    repack,
    slot_pick,
    row_place,
    column_place,
    slot_place,
    dispatch_send,
    dispatch_recv,
    partner_rows,
    combine_send,
    combine_recv,
    half_send,
    half_own,
    half_recv,
    gate_send,
    gate_recv,
    rows_in,
    squares,
    gate_saved,
    up_saved,
    hidden_grad,
    picked,
    kept,
    stats,
    weight_sem,
    act_sem,
    grad_sem,
    pipe_sem,
    dispatch_send_sem,
    dispatch_recv_sem,
    swap_send_sem,
    swap_recv_sem,
    half_send_sem,
    half_recv_sem,
    combine_send_sem,
    combine_recv_sem,
    gate_send_sem,
    gate_recv_sem,
):
    sections, micro_count, chips, capacity = geometry
    lines, columns = grid_of(chips)
    tokens, width = acts.shape[1], acts.shape[2]
    piece = width // sum(CHUNK_PIECES)
    group = chips * capacity
    slots = gate_send.shape[2]
    hidden = wg.shape[1]
    experts = router_ref.shape[0]
    bf16, f32 = jnp.bfloat16, jnp.float32
    section = lax.axis_index("pipe")
    place = lax.axis_index("expert")
    core = lax.rem(place, 2)
    chip = place // 2
    line, column = chip // columns, lax.rem(chip, columns)
    partner = chip * 2 + (1 - core)
    others = pl.ds(1, chips - 1)

    def peer(step, sign, to_core=core):
        to_line = lax.rem(line + sign * (step // columns) + lines, lines)
        to_column = lax.rem(column + sign * lax.rem(step, columns) + columns, columns)
        return {"expert": (to_line * columns + to_column) * 2 + to_core}

    def begin_of(c, q=0):
        return (sum(CHUNK_PIECES[:c]) + q) * piece

    def span(c):
        return slice(begin_of(c), begin_of(c + 1))

    def pieces_of(value):
        return [value[:, q : q + piece] for q in range(0, value.shape[1], piece)]

    def block_of(c):
        return block_rows(c, capacity)

    barrier = pltpu.get_barrier_semaphore()

    def greet(step, carry):
        for to_core in (core, 1 - core):
            pl.semaphore_signal(
                barrier, inc=1, device_id=peer(step, 1, to_core), device_id_type=MESH
            )
        return carry

    weights = [
        pltpu.make_async_copy(source, target, weight_sem.at[i])
        for i, (source, target) in enumerate([(wg_hbm, wg), (wu_hbm, wu), (wd_hbm, wd)])
    ]

    def fetch(source, target, semaphore):
        for m in range(micro_count):
            for c in range(CHUNKS):
                pltpu.make_async_copy(
                    source.at[m, :, span(c)],
                    target.at[m, :, span(c)],
                    semaphore.at[m * CHUNKS + c],
                ).start()

    @pl.when(section == 0)
    def _():
        fetch(inputs_ref, acts, act_sem)

    @pl.when(section == sections - 1)
    def _():
        fetch(cotangent_ref, grads, grad_sem)

    for copy in weights:
        copy.start()
    lax.fori_loop(1, chips, greet, 0)
    pl.semaphore_signal(barrier, inc=1, device_id={"expert": partner}, device_id_type=MESH)
    for sign in (1, sections - 1):
        pl.semaphore_signal(
            barrier,
            inc=1,
            device_id={"pipe": lax.rem(section + sign, sections)},
            device_id_type=MESH,
        )

    def iota(shape, axis):
        return lax.broadcasted_iota(jnp.int32, shape, axis)

    def hot(condition):
        return jnp.where(condition, 1.0, 0.0).astype(bf16)

    for c in range(CHUNKS):

        def place_of(number):
            within = lax.rem(number, block_of(c))
            q = within // capacity
            row = q * group + (number // block_of(c)) * capacity + lax.rem(within, capacity)
            return jnp.where(within < CHUNK_PIECES[c] * capacity, row, -1)

        shape = (CHUNK_PIECES[c] * group, chips * block_of(c))
        unpack[c][...] = hot(iota(shape, 0) == place_of(iota((1, shape[1]), 1)))
        repack[c][...] = hot(iota(shape[::-1], 1) == place_of(iota((shape[1], 1), 0)))
    shape = (group, chips * slots)
    wanted = iota((group, 1), 0)
    wanted = (wanted // capacity) * slots + lax.rem(wanted, capacity)
    slot_pick[...] = hot(iota(shape, 1) == wanted)

    earlier = hot(iota((tokens, tokens), 0) < iota((tokens, tokens), 1))
    for m in range(micro_count):
        ids = ids_ref[m]
        found = [hot(iota((experts, tokens), 0) == ids[k : k + 1]) for k in range(2)]
        counts = matmul(found[0] + found[1], earlier)
        ranks = [
            jnp.sum(counts * found[k].astype(f32), axis=0, keepdims=True) for k in range(2)
        ]
        ranks = jnp.concatenate(ranks, axis=0)
        to_line = lax.rem(ids // columns - line + lines, lines)
        to_column = lax.rem(lax.rem(ids, columns) - column + columns, columns)
        steps_to = (to_line * columns + to_column).astype(f32).astype(bf16)
        ranks_to = ranks.astype(bf16)
        for c in range(CHUNKS):
            lanes = CHUNK_PIECES[c] * tokens
            across = hot(iota((tokens, lanes), 0) == lax.rem(iota((1, lanes), 1), tokens))
            down = hot(lax.rem(iota((lanes, 1), 0), tokens) == iota((lanes, tokens), 1))
            where = matmul(steps_to, across).astype(jnp.int32) * block_of(c)
            where += matmul(ranks_to, across).astype(jnp.int32)
            row_place[c][m] = where + (iota((1, lanes), 1) // tokens) * capacity
            where = matmul_t(down, steps_to).astype(jnp.int32) * block_of(c)
            where += matmul_t(down, ranks_to).astype(jnp.int32)
            column_place[c][m] = where + (iota((lanes, 1), 0) // tokens) * capacity
        slot_place[m] = (steps_to.astype(f32) * slots + ranks).astype(jnp.int32)

    pl.semaphore_wait(barrier, 2 * (chips - 1) + 1 + 2)

    def wait_all(buffer, semaphore):
        pltpu.make_async_copy(buffer, buffer, semaphore).wait()

    def post(values, m, c, send, recv, send_sem, recv_sem, sign):
        values = values.astype(bf16).reshape(chips, block_of(c), piece)
        recv[m, 0] = values[0]
        send[m, others] = values[1:]

        def start(step, carry):
            pltpu.make_async_remote_copy(
                src_ref=send.at[m, step],
                dst_ref=recv.at[m, step],
                send_sem=send_sem.at[m * CHUNKS + c],
                recv_sem=recv_sem.at[m * CHUNKS + c],
                device_id=peer(step, sign),
                device_id_type=MESH,
            ).start()
            return carry

        lax.fori_loop(1, chips, start, 0)

    def dispatch(stacked, m, c, way):
        target = row_place[c][m]
        rows = iota((chips * block_of(c), target.shape[1]), 0)
        table = hot(rows == target[0:1]) + hot(rows == target[1:2])
        post(
            matmul(table, stacked),
            m,
            c,
            dispatch_send[way][c],
            dispatch_recv[way][c],
            dispatch_send_sem.at[way],
            dispatch_recv_sem.at[way],
            1,
        )

    def expert_hot(m):
        same = hot(iota((tokens, tokens), 0) == iota((tokens, tokens), 1))
        names = matmul_t(same, ids_ref[m].astype(f32).astype(bf16)).astype(jnp.int32)
        return [
            jnp.where(iota((tokens, experts), 1) == names[:, k : k + 1], 1.0, 0.0)
            for k in range(2)
        ]

    def take_rows(m, c, way):
        number = m * CHUNKS + c
        send, recv = dispatch_send[way][c], dispatch_recv[way][c]
        wait_all(recv.at[m, others], dispatch_recv_sem.at[way, number])
        swap = pltpu.make_async_remote_copy(
            src_ref=recv.at[m],
            dst_ref=partner_rows[way][c].at[m],
            send_sem=swap_send_sem,
            recv_sem=swap_recv_sem.at[way, number],
            device_id={"expert": partner},
            device_id_type=MESH,
        )
        swap.start()
        wait_all(send.at[m, others], dispatch_send_sem.at[way, number])
        for part, source in enumerate((recv, partner_rows[way][c])):
            if part == 1:
                swap.wait()
            rows = matmul(unpack[c][...], source[m].reshape(chips * block_of(c), piece))
            mine = slice(part * group, (part + 1) * group)
            square = jnp.zeros((group, piece), f32)
            for q in range(CHUNK_PIECES[c]):
                at = slice(begin_of(c, q), begin_of(c, q + 1))
                found = rows[q * group : (q + 1) * group]
                if way == 0:
                    square += found * found
                    found = found * gain_ref[:, at]
                rows_in[way, mine, at] = found.astype(bf16)
            if way == 0:
                square = jnp.sum(square, axis=1, keepdims=True)
                squares[mine] = square if c == 0 else squares[mine] + square

    def halves_and_combine(m, way, product):
        copies = []
        for c in range(CHUNKS):
            part = product(c).astype(bf16)
            for q, values in enumerate(pieces_of(part)):
                half_own[c][q] = values[:group]
                half_send[c][q] = values[group:]
            copy = pltpu.make_async_remote_copy(
                src_ref=half_send[c],
                dst_ref=half_recv[way][c].at[m],
                send_sem=half_send_sem.at[c],
                recv_sem=half_recv_sem.at[way, m * CHUNKS + c],
                device_id={"expert": partner},
                device_id_type=MESH,
            )
            copy.start()
            copies.append(copy)
        for c in range(CHUNKS):
            copies[c].wait()
            total = half_own[c][...].astype(f32) + half_recv[way][c][m].astype(f32)
            total = total.astype(bf16).reshape(CHUNK_PIECES[c] * group, piece)
            post(
                matmul(repack[c][...], total),
                m,
                c,
                combine_send[way][c],
                combine_recv[way][c],
                combine_send_sem.at[way],
                combine_recv_sem.at[way],
                -1,
            )

    def send_gates(m, gates):
        target = slot_place[m]
        rows = iota((chips * slots, tokens), 0)
        tables = [hot(rows == target[k : k + 1]) for k in range(2)]
        spread = jnp.zeros((chips * slots, 128), f32)
        for k in range(2):
            value = jnp.broadcast_to(gates[k], (tokens, 128))
            high = value.astype(bf16)
            low = (value - high.astype(f32)).astype(bf16)
            spread += matmul(tables[k], high) + matmul(tables[k], low)
        spread = spread.reshape(chips, slots, 128)
        gate_send[m] = spread
        gate_recv[m, 0, 0] = spread[0]

        def copy_to(step, part):
            pltpu.make_async_remote_copy(
                src_ref=gate_send.at[m, step],
                dst_ref=gate_recv.at[m, part, step],
                send_sem=gate_send_sem.at[m, part],
                recv_sem=gate_recv_sem.at[m, part],
                device_id=peer(step, 1, core if part == 0 else 1 - core),
                device_id_type=MESH,
            ).start()

        def start(step, carry):
            copy_to(step, 0)
            copy_to(step, 1)
            return carry

        copy_to(0, 1)
        lax.fori_loop(1, chips, start, 0)

    def take_gates(m):
        gates = []
        for part, arrived in enumerate((others, pl.ds(0, chips))):
            wait_all(gate_recv.at[m, part, arrived], gate_recv_sem.at[m, part])
            wait_all(gate_send.at[m, arrived], gate_send_sem.at[m, part])
            value = gate_recv[m, part].reshape(chips * slots, 128)
            high = value.astype(bf16)
            low = (value - high.astype(f32)).astype(bf16)
            gates.append(matmul(slot_pick[...], high) + matmul(slot_pick[...], low))
        return jnp.concatenate(gates, axis=0)[:, :1]

    def forward_send(m, c):
        wait_all(acts.at[m, :, span(c)], act_sem.at[m * CHUNKS + c])
        dispatch(jnp.concatenate(pieces_of(acts[m, :, span(c)]), axis=0), m, c, 0)
        if c < CHUNKS - 1:
            return
        wide_in = acts[m].astype(f32)
        scale = lax.rsqrt(jnp.mean(wide_in * wide_in, axis=1, keepdims=True) + EPSILON)
        normed = (wide_in * scale * gain_ref[...]).astype(bf16)
        logits = matmul_t(normed, router_ref[...])
        chances = [
            1.0 / (1.0 + jnp.exp(-jnp.sum(logits * named, axis=1, keepdims=True)))
            for named in expert_hot(m)
        ]
        total = chances[0] + chances[1]
        gates = [chance / total for chance in chances]
        send_gates(m, gates)
        stats[m, 0] = scale
        for k in range(2):
            stats[m, 1 + k] = chances[k]
            stats[m, 3 + k] = gates[k]

    def forward_expert(m, c):
        if c == 0:

            @pl.when(m == 0)
            def _():
                for copy in weights:
                    copy.wait()

        take_rows(m, c, 0)
        gate_pre = matmul(rows_in[0, :, span(c)], wg[span(c)])
        up_pre = matmul(rows_in[0, :, span(c)], wu[span(c)])
        if c > 0:
            gate_pre += gate_saved[m]
            up_pre += up_saved[m]
        if c < CHUNKS - 1:
            gate_saved[m] = gate_pre
            up_saved[m] = up_pre
            return
        scale = lax.rsqrt(squares[...] / width + EPSILON)
        gate_pre = gate_pre * scale
        up_pre = up_pre * scale
        gate_saved[m] = gate_pre
        up_saved[m] = up_pre
        inner = (gate_pre / (1.0 + jnp.exp(-gate_pre)) * up_pre).astype(bf16)
        halves_and_combine(m, 0, lambda d: matmul(inner, wd[:, span(d)]))

    def receive_combined(m, c, way):
        number = m * CHUNKS + c
        recv = combine_recv[way][c]
        wait_all(recv.at[m, others], combine_recv_sem.at[way, number])
        wait_all(combine_send[way][c].at[m, others], combine_send_sem.at[way, number])
        return recv[m].reshape(chips * block_of(c), piece)

    def column_tables(m, c):
        target = column_place[c][m]
        places = iota((target.shape[0], chips * block_of(c)), 1)
        return [hot(places == target[:, k : k + 1]) for k in range(2)]

    def forward_finish(m, c):
        received = receive_combined(m, c, 0)
        found = [matmul(table, received) for table in column_tables(m, c)]
        for q in range(CHUNK_PIECES[c]):
            at = slice(begin_of(c, q), begin_of(c, q + 1))
            total = acts[m, :, at].astype(f32)
            for k in range(2):
                rows = found[k][q * tokens : (q + 1) * tokens]
                picked[m, k, :, at] = rows.astype(bf16)
                total += stats[m, 3 + k] * rows
            out_ref[m, :, at] = total.astype(bf16)

        @pl.when(section < sections - 1)
        def _():
            pltpu.make_async_remote_copy(
                src_ref=out_ref.at[m, :, span(c)],
                dst_ref=acts.at[m, :, span(c)],
                send_sem=pipe_sem.at[0],
                recv_sem=act_sem.at[m * CHUNKS + c],
                device_id={"pipe": section + 1},
                device_id_type=MESH,
            ).start()

    def backward_send(m, c):
        wait_all(grads.at[m, :, span(c)], grad_sem.at[m * CHUNKS + c])
        dispatch(jnp.concatenate(pieces_of(grads[m, :, span(c)]), axis=0), m, c, 1)

    def backward_expert(m, c):
        take_rows(m, c, 1)
        inner_grad = matmul_t(rows_in[1, :, span(c)], wd[:, span(c)])
        if c > 0:
            inner_grad += hidden_grad[...]
        if c < CHUNKS - 1:
            hidden_grad[...] = inner_grad
            return
        inner_grad = inner_grad * take_gates(m)
        gate_pre = gate_saved[m]
        sigmoid = 1.0 / (1.0 + jnp.exp(-gate_pre))
        pre_grad = (
            inner_grad * up_saved[m] * sigmoid * (1.0 + gate_pre * (1.0 - sigmoid))
        ).astype(bf16)
        up_grad = (inner_grad * gate_pre * sigmoid).astype(bf16)
        halves_and_combine(
            m, 1, lambda d: matmul_t(pre_grad, wg[span(d)]) + matmul_t(up_grad, wu[span(d)])
        )

    def score_slopes(m):
        upstream = grads[m].astype(f32)
        slopes = [
            jnp.sum(upstream * picked[m, k].astype(f32), axis=1, keepdims=True)
            for k in range(2)
        ]
        weighted = stats[m, 3] * slopes[0] + stats[m, 4] * slopes[1]
        total = stats[m, 1] + stats[m, 2]
        for k in range(2):
            chance = stats[m, 1 + k]
            stats[m, 5 + k] = (slopes[k] - weighted) / total * chance * (1.0 - chance)

    def backward_finish(m, c):
        if c == 0:
            score_slopes(m)
        named = expert_hot(m)
        router_table = (stats[m, 5] * named[0] + stats[m, 6] * named[1]).astype(bf16)
        routed = matmul(router_table, router_ref[:, span(c)])
        received = receive_combined(m, c, 1)
        tables = column_tables(m, c)
        summed = matmul(tables[0] + tables[1], received)
        inner = jnp.zeros((tokens, piece), f32)
        for q in range(CHUNK_PIECES[c]):
            at = slice(begin_of(c, q), begin_of(c, q + 1))
            near = slice(q * piece, (q + 1) * piece)
            normed_grad = summed[q * tokens : (q + 1) * tokens] + routed[:, near]
            normed_grad = normed_grad * gain_ref[:, at]
            inner += acts[m, :, at].astype(f32) * normed_grad
            kept[:, at] = normed_grad
        inner = jnp.sum(inner, axis=1, keepdims=True)
        if c > 0:
            inner += stats[m, 7]
        if c < CHUNKS - 1:
            stats[m, 7] = inner
            return
        scale = stats[m, 0]
        inner = scale * scale * scale * (inner / width)
        for d in range(CHUNKS):
            result = grads[m, :, span(d)].astype(f32) + scale * kept[:, span(d)]
            result -= acts[m, :, span(d)].astype(f32) * inner
            grad_ref[m, :, span(d)] = result.astype(bf16)

            @pl.when(section > 0)
            def _():
                pltpu.make_async_remote_copy(
                    src_ref=grad_ref.at[m, :, span(d)],
                    dst_ref=grads.at[m, :, span(d)],
                    send_sem=pipe_sem.at[1],
                    recv_sem=grad_sem.at[m * CHUNKS + d],
                    device_id={"pipe": section - 1},
                    device_id_type=MESH,
                ).start()

    steps = (
        forward_send,
        forward_expert,
        forward_finish,
        backward_send,
        backward_expert,
        backward_finish,
    )
    words = order_words(sections, micro_count)

    def run(i, counts):
        word = jnp.int32(0)
        for s, row in enumerate(words):
            for w, number in enumerate(row):
                word = jnp.where((section == s) & (i // DIGITS == w), number, word)
        word = lax.fori_loop(0, lax.rem(i, DIGITS), lambda j, rest: rest // 8, word)
        kind = lax.rem(word, 8)
        for number, step in enumerate(steps):
            m, c = counts[number] // CHUNKS, lax.rem(counts[number], CHUNKS)
            for d in range(CHUNKS):

                @pl.when((kind == number) & (c == d))
                def _():
                    step(m, d)

        return tuple(
            count + jnp.where(kind == number, 1, 0) for number, count in enumerate(counts)
        )

    total_steps = 6 * micro_count * CHUNKS
    lax.fori_loop(0, total_steps, run, (jnp.int32(0),) * 6)

    @pl.when(section < sections - 1)
    def _():
        wait_all(out_ref, pipe_sem.at[0])

    @pl.when(section > 0)
    def _():
        wait_all(grad_ref, pipe_sem.at[1])


KINDS = "abcABC"
DIGITS = 10
ORDERS = (
    "aaaabbbbcaacaaccbbbbccccAAABABBBCCCCAAAABBBBCCCC",
    "aaababbbccccaaaabbbbccccAAABABBBCCCCAAAABBBBCCCC",
    "aaababbbccccaaaabbbbccccAAABABBBCCCCAAABABBBCCCC",
    "AAAAAAAAaaaabbBBbbBBaaccCCccCaaCbbBBbcbBBcCcCcCC",
)


def order_words(sections, micro_count):
    orders = ORDERS
    if (sections, micro_count) != (4, 4):
        orders = ("aabbcc" * micro_count + "AABBCC" * micro_count,) * (sections - 1)
        orders += ("AA" * micro_count + "aabbcc" * micro_count + "BBCC" * micro_count,)
    words = []
    for order in orders:
        row = []
        for begin in range(0, len(order), DIGITS):
            digits = [KINDS.index(kind) for kind in order[begin : begin + DIGITS]]
            row.append(sum(digit * 8**j for j, digit in enumerate(digits)))
        words.append(row)
    return words


def on_device(
    inputs, cotangent, norm_gain, router_weight, gate_weight, up_weight, down_weight, route_ids
):
    sections = lax.axis_size("pipe")
    chips = lax.axis_size("expert") // 2
    micro_count, tokens, width = inputs.shape
    experts = router_weight.shape[2]
    top_count = route_ids.shape[3]
    capacity = min(tokens, (5 * tokens * top_count + 4 * experts - 1) // (4 * experts))
    hidden = gate_weight.shape[2]
    piece = width // sum(CHUNK_PIECES)
    group = chips * capacity
    slots = -(-capacity // 8) * 8
    anywhere = pl.BlockSpec(memory_space=pl.ANY)
    inside = pl.BlockSpec(memory_space=pltpu.VMEM)
    bf16, f32 = jnp.bfloat16, jnp.float32
    out = jax.ShapeDtypeStruct((micro_count, tokens, width), bf16)
    dma = pltpu.SemaphoreType.DMA
    geometry = (sections, micro_count, chips, capacity)

    def per_chunk(shape_of, ways=0):
        chunks = tuple(pltpu.VMEM(shape_of(c), bf16) for c in range(CHUNKS))
        return (chunks, chunks) if ways else chunks

    def rows_of(c):
        return CHUNK_PIECES[c] * group

    def blocks_of(c):
        return chips * block_rows(c, capacity)

    def lanes_of(c):
        return CHUNK_PIECES[c] * tokens

    def exchange(c):
        return (micro_count, chips, block_rows(c, capacity), piece)

    def halves(c):
        return (CHUNK_PIECES[c], group, piece)

    def places(shape_of):
        return tuple(pltpu.VMEM(shape_of(c), jnp.int32) for c in range(CHUNKS))

    parts = micro_count * CHUNKS
    forward_out, backward_out = pl.pallas_call(
        functools.partial(relay_kernel, geometry),
        out_shape=(out, out),
        in_specs=[anywhere] * 2 + [inside] * 2 + [anywhere] * 3 + [inside],
        out_specs=(inside, inside),
        scratch_shapes=[
            pltpu.VMEM((width, hidden), bf16),
            pltpu.VMEM((width, hidden), bf16),
            pltpu.VMEM((hidden, width), bf16),
            pltpu.VMEM((micro_count, tokens, width), bf16),
            pltpu.VMEM((micro_count, tokens, width), bf16),
            per_chunk(lambda c: (rows_of(c), blocks_of(c))),
            per_chunk(lambda c: (blocks_of(c), rows_of(c))),
            pltpu.VMEM((group, chips * slots), bf16),
            places(lambda c: (micro_count, top_count, lanes_of(c))),
            places(lambda c: (micro_count, lanes_of(c), top_count)),
            pltpu.VMEM((micro_count, top_count, tokens), jnp.int32),
            per_chunk(exchange, 2),
            per_chunk(exchange, 2),
            per_chunk(exchange, 2),
            per_chunk(exchange, 2),
            per_chunk(exchange, 2),
            per_chunk(halves),
            per_chunk(halves),
            per_chunk(lambda c: (micro_count, *halves(c)), 2),
            pltpu.VMEM((micro_count, chips, slots, 128), f32),
            pltpu.VMEM((micro_count, 2, chips, slots, 128), f32),
            pltpu.VMEM((2, 2 * group, width), bf16),
            pltpu.VMEM((2 * group, 1), f32),
            pltpu.VMEM((micro_count, 2 * group, hidden), f32),
            pltpu.VMEM((micro_count, 2 * group, hidden), f32),
            pltpu.VMEM((2 * group, hidden), f32),
            pltpu.VMEM((micro_count, top_count, tokens, width), bf16),
            pltpu.VMEM((tokens, width), f32),
            pltpu.VMEM((micro_count, 8, tokens, 1), f32),
            dma((3,)),
            dma((parts,)),
            dma((parts,)),
            dma((2,)),
            dma((2, parts)),
            dma((2, parts)),
            dma,
            dma((2, parts)),
            dma((CHUNKS,)),
            dma((2, parts)),
            dma((2, parts)),
            dma((2, parts)),
            dma((micro_count, 2)),
            dma((micro_count, 2)),
        ],
        compiler_params=pltpu.CompilerParams(
            collective_id=0, has_side_effects=True, vmem_limit_bytes=66_000_000
        ),
    )(
        inputs,
        cotangent,
        norm_gain,
        router_weight[0].T,
        gate_weight[0],
        up_weight[0],
        down_weight[0],
        jnp.moveaxis(route_ids[0], 2, 1),
    )
    return (forward_out[None], backward_out[None])


def solution(mesh):
    return jax.shard_map(
        on_device,
        mesh=mesh,
        in_specs=(
            P(None, "expert", None),
            P(None, "expert", None),
            P("pipe", None),
            P("pipe", None, None),
            P("pipe", None, "expert"),
            P("pipe", None, "expert"),
            P("pipe", "expert", None),
            P("pipe", None, "expert", None),
        ),
        out_specs=(P("pipe", None, "expert", None), P("pipe", None, "expert", None)),
        check_vma=False,
    )
```

time: 370 us -> 329 us (0.89)
  Pallas kernels: 357 us -> 323 us
  local copies, waits for them, and re-layouts: 10.1 us -> 4.32 us
    pallas_call x1, Pallas kernels: 357 us -> 323 us  [on_device(): pl.pallas_call(functools.partial(relay_kernel, geometry), out_shape=(out,...]
where the time goes in v3:
time: 329 us; the launch traced here: 328 us
  Pallas kernels  323 us (98%)
  local copies, waits for them, and re-layouts  4.32 us (1%)
    pallas_call x1, Pallas kernels, on_device(): pl.pallas_call(functools.partial(relay_kernel, geometry), out_shape=(out,...  323 us

profile of v3, /device:TPU:1, one launch (start us, length us, event | category | flops | bytes accessed | tf_op | source)
XLA Modules:
  0.0 328.4 jit_solution(16872126955923356381)
XLA Ops:
  0.6 323.4 %shard_map.95 = (bf16[4,32,3584]{2,1,0:T(8,128)(2,1)}, bf16[4,32,3584]{2,1,0:T(8,128)(2,1)}) custom-call(bf16[4,32,3584]{2,1,0:T(8,128)(2,1)} %inputs_ref.1, bf16[4,32,3584]{2,1,0:T(8,128)(2,1)} %cotangent_ref.1, f32[1,3584]{1,0:T(1,128)} %gain_ref.1, bf16[16,3584]{1,0:T(8,128)(2,1)} %bitcast.16, bf16[3584,512]{1,0:T(8,128)(2,1)} %bitcast.11, ...), custom_call_target="tpu_custom_call" | custom-call | tf_op jit(solution)/shard_map/pallas_call | solution.py:637
  324.1 2.2 copy.12
  326.2 2.2 copy.13

commit v4 on v3

--- a/solution.py
+++ b/solution.py
@@ -72,7 +72,7 @@
     squares,
     gate_saved,
     up_saved,
-    hidden_grad,
+    gate_rows,
     picked,
     kept,
     stats,
@@ -261,36 +261,47 @@
             for k in range(2)
         ]
 
-    def take_rows(m, c, way):
-        number = m * CHUNKS + c
-        send, recv = dispatch_send[way][c], dispatch_recv[way][c]
-        wait_all(recv.at[m, others], dispatch_recv_sem.at[way, number])
-        swap = pltpu.make_async_remote_copy(
-            src_ref=recv.at[m],
-            dst_ref=partner_rows[way][c].at[m],
-            send_sem=swap_send_sem,
-            recv_sem=swap_recv_sem.at[way, number],
-            device_id={"expert": partner},
-            device_id_type=MESH,
-        )
-        swap.start()
-        wait_all(send.at[m, others], dispatch_send_sem.at[way, number])
-        for part, source in enumerate((recv, partner_rows[way][c])):
-            if part == 1:
-                swap.wait()
-            rows = matmul(unpack[c][...], source[m].reshape(chips * block_of(c), piece))
-            mine = slice(part * group, (part + 1) * group)
-            square = jnp.zeros((group, piece), f32)
-            for q in range(CHUNK_PIECES[c]):
-                at = slice(begin_of(c, q), begin_of(c, q + 1))
-                found = rows[q * group : (q + 1) * group]
-                if way == 0:
-                    square += found * found
-                    found = found * gain_ref[:, at]
-                rows_in[way, mine, at] = found.astype(bf16)
+    def unpack_rows(source, m, c, way, part):
+        rows = matmul(unpack[c][...], source[m].reshape(chips * block_of(c), piece))
+        mine = slice(part * group, (part + 1) * group)
+        square = jnp.zeros((group, piece), f32)
+        for q in range(CHUNK_PIECES[c]):
+            at = slice(begin_of(c, q), begin_of(c, q + 1))
+            found = rows[q * group : (q + 1) * group]
             if way == 0:
-                square = jnp.sum(square, axis=1, keepdims=True)
-                squares[mine] = square if c == 0 else squares[mine] + square
+                square += found * found
+                found = found * gain_ref[:, at]
+            rows_in[way, mine, at] = found.astype(bf16)
+        if way == 0:
+            square = jnp.sum(square, axis=1, keepdims=True)
+            squares[mine] = square if c == 0 else squares[mine] + square
+
+    def take_rows(m, way, meanwhile, product):
+        swaps = []
+        for c in range(CHUNKS):
+            number = m * CHUNKS + c
+            send, recv = dispatch_send[way][c], dispatch_recv[way][c]
+            wait_all(recv.at[m, others], dispatch_recv_sem.at[way, number])
+            swap = pltpu.make_async_remote_copy(
+                src_ref=recv.at[m],
+                dst_ref=partner_rows[way][c].at[m],
+                send_sem=swap_send_sem.at[c],
+                recv_sem=swap_recv_sem.at[way, number],
+                device_id={"expert": partner},
+                device_id_type=MESH,
+            )
+            swap.start()
+            swaps.append(swap)
+            wait_all(send.at[m, others], dispatch_send_sem.at[way, number])
+            unpack_rows(recv, m, c, way, 0)
+        meanwhile()
+        total = None
+        for c in range(CHUNKS):
+            swaps[c].wait()
+            unpack_rows(partner_rows[way][c], m, c, way, 1)
+            found = product(c)
+            total = found if total is None else [a + b for a, b in zip(total, found)]
+        return total
 
     def halves_and_combine(m, way, product):
         copies = []
@@ -388,24 +399,17 @@
             stats[m, 1 + k] = chances[k]
             stats[m, 3 + k] = gates[k]
 
-    def forward_expert(m, c):
-        if c == 0:
-
-            @pl.when(m == 0)
-            def _():
-                for copy in weights:
-                    copy.wait()
-
-        take_rows(m, c, 0)
-        gate_pre = matmul(rows_in[0, :, span(c)], wg[span(c)])
-        up_pre = matmul(rows_in[0, :, span(c)], wu[span(c)])
-        if c > 0:
-            gate_pre += gate_saved[m]
-            up_pre += up_saved[m]
-        if c < CHUNKS - 1:
-            gate_saved[m] = gate_pre
-            up_saved[m] = up_pre
-            return
+    def forward_expert(m):
+        @pl.when(m == 0)
+        def _():
+            for copy in weights:
+                copy.wait()
+
+        def product(c):
+            rows = rows_in[0, :, span(c)]
+            return [matmul(rows, wg[span(c)]), matmul(rows, wu[span(c)])]
+
+        gate_pre, up_pre = take_rows(m, 0, lambda: None, product)
         scale = lax.rsqrt(squares[...] / width + EPSILON)
         gate_pre = gate_pre * scale
         up_pre = up_pre * scale
@@ -453,15 +457,14 @@
         wait_all(grads.at[m, :, span(c)], grad_sem.at[m * CHUNKS + c])
         dispatch(jnp.concatenate(pieces_of(grads[m, :, span(c)]), axis=0), m, c, 1)
 
-    def backward_expert(m, c):
-        take_rows(m, c, 1)
-        inner_grad = matmul_t(rows_in[1, :, span(c)], wd[:, span(c)])
-        if c > 0:
-            inner_grad += hidden_grad[...]
-        if c < CHUNKS - 1:
-            hidden_grad[...] = inner_grad
-            return
-        inner_grad = inner_grad * take_gates(m)
+    def backward_expert(m):
+        def load_gates():
+            gate_rows[...] = take_gates(m)
+
+        (inner_grad,) = take_rows(
+            m, 1, load_gates, lambda c: [matmul_t(rows_in[1, :, span(c)], wd[:, span(c)])]
+        )
+        inner_grad = inner_grad * gate_rows[...]
         gate_pre = gate_saved[m]
         sigmoid = 1.0 / (1.0 + jnp.exp(-gate_pre))
         pre_grad = (
@@ -535,14 +538,22 @@
     )
     words = order_words(sections, micro_count)
 
-    def run(i, counts):
-        word = jnp.int32(0)
-        for s, row in enumerate(words):
-            for w, number in enumerate(row):
-                word = jnp.where((section == s) & (i // DIGITS == w), number, word)
-        word = lax.fori_loop(0, lax.rem(i, DIGITS), lambda j, rest: rest // 8, word)
+    def run(i, carry):
+        word, *counts = carry
+        for w in range(len(words[0])):
+            fresh = jnp.int32(0)
+            for s, row in enumerate(words):
+                fresh += jnp.where(section == s, row[w], 0)
+            word = jnp.where(i == w * DIGITS, fresh, word)
         kind = lax.rem(word, 8)
         for number, step in enumerate(steps):
+            if number in WHOLE:
+
+                @pl.when(kind == number)
+                def _():
+                    step(counts[number])
+
+                continue
             m, c = counts[number] // CHUNKS, lax.rem(counts[number], CHUNKS)
             for d in range(CHUNKS):
 
@@ -550,12 +561,11 @@
                 def _():
                     step(m, d)
 
-        return tuple(
-            count + jnp.where(kind == number, 1, 0) for number, count in enumerate(counts)
-        )
-
-    total_steps = 6 * micro_count * CHUNKS
-    lax.fori_loop(0, total_steps, run, (jnp.int32(0),) * 6)
+        counts = [count + jnp.where(kind == n, 1, 0) for n, count in enumerate(counts)]
+        return (word // 8, *counts)
+
+    total_steps = micro_count * (4 * CHUNKS + 2)
+    lax.fori_loop(0, total_steps, run, (jnp.int32(0),) * 7)
 
     @pl.when(section < sections - 1)
     def _():
@@ -567,20 +577,21 @@
 
 
 KINDS = "abcABC"
+WHOLE = (1, 4)
 DIGITS = 10
 ORDERS = (
-    "aaaabbbbcaacaaccbbbbccccAAABABBBCCCCAAAABBBBCCCC",
-    "aaababbbccccaaaabbbbccccAAABABBBCCCCAAAABBBBCCCC",
-    "aaababbbccccaaaabbbbccccAAABABBBCCCCAAABABBBCCCC",
-    "AAAAAAAAaaaabbBBbbBBaaccCCccCaaCbbBBbcbBBcCcCcCC",
+    "aaabcacabcacbccaabccAABAACBAACBCACACCBCC",
+    "aabacacbaaccbccaabccAABCACABCAACBAACCBCC",
+    "aabcacabaaccbcacAAaBbCCAAccBAACCBCAACBCC",
+    "AAAAAaabBacacCAACbaaBccbCCBccaCaCAbBccCC",
 )
 
 
 def order_words(sections, micro_count):
     orders = ORDERS
     if (sections, micro_count) != (4, 4):
-        orders = ("aabbcc" * micro_count + "AABBCC" * micro_count,) * (sections - 1)
-        orders += ("AA" * micro_count + "aabbcc" * micro_count + "BBCC" * micro_count,)
+        orders = ("aabcc" * micro_count + "AABCC" * micro_count,) * (sections - 1)
+        orders += ("AA" * micro_count + "aabcc" * micro_count + "BCC" * micro_count,)
     words = []
     for order in orders:
         row = []
@@ -665,7 +676,7 @@
             pltpu.VMEM((2 * group, 1), f32),
             pltpu.VMEM((micro_count, 2 * group, hidden), f32),
             pltpu.VMEM((micro_count, 2 * group, hidden), f32),
-            pltpu.VMEM((2 * group, hidden), f32),
+            pltpu.VMEM((2 * group, 1), f32),
             pltpu.VMEM((micro_count, top_count, tokens, width), bf16),
             pltpu.VMEM((tokens, width), f32),
             pltpu.VMEM((micro_count, 8, tokens, 1), f32),
@@ -675,7 +686,7 @@
             dma((2,)),
             dma((2, parts)),
             dma((2, parts)),
-            dma,
+            dma((CHUNKS,)),
             dma((2, parts)),
             dma((CHUNKS,)),
             dma((2, parts)),

time: 329 us -> 318 us (0.967)
  Pallas kernels: 323 us -> 312 us
    pallas_call x1, Pallas kernels: 323 us -> 312 us  [on_device(): pl.pallas_call(functools.partial(relay_kernel, geometry), out_shape=(out,...]
where the time goes in v4:
time: 318 us; the launch traced here: 317 us
  Pallas kernels  312 us (98%)
  local copies, waits for them, and re-layouts  4.32 us (1%)
    pallas_call x1, Pallas kernels, on_device(): pl.pallas_call(functools.partial(relay_kernel, geometry), out_shape=(out,...  312 us

profile of v4, /device:TPU:1, one launch (start us, length us, event | category | flops | bytes accessed | tf_op | source)
XLA Modules:
  0.0 317.4 jit_solution(309054185257753450)
XLA Ops:
  0.6 312.4 %shard_map.95 = (bf16[4,32,3584]{2,1,0:T(8,128)(2,1)}, bf16[4,32,3584]{2,1,0:T(8,128)(2,1)}) custom-call(bf16[4,32,3584]{2,1,0:T(8,128)(2,1)} %inputs_ref.1, bf16[4,32,3584]{2,1,0:T(8,128)(2,1)} %cotangent_ref.1, f32[1,3584]{1,0:T(1,128)} %gain_ref.1, bf16[16,3584]{1,0:T(8,128)(2,1)} %bitcast.16, bf16[3584,512]{1,0:T(8,128)(2,1)} %bitcast.11, ...), custom_call_target="tpu_custom_call" | custom-call | tf_op jit(solution)/shard_map/pallas_call | solution.py:648
  313.1 2.2 copy.12
  315.2 2.2 copy.13

commit v5 on v4

--- a/solution.py
+++ b/solution.py
@@ -96,6 +96,7 @@
     tokens, width = acts.shape[1], acts.shape[2]
     piece = width // sum(CHUNK_PIECES)
     group = chips * capacity
+    half_group, half_chips = group // 2, chips // 2
     slots = gate_send.shape[2]
     hidden = wg.shape[1]
     experts = router_ref.shape[0]
@@ -173,22 +174,6 @@
 
     def hot(condition):
         return jnp.where(condition, 1.0, 0.0).astype(bf16)
-
-    for c in range(CHUNKS):
-
-        def place_of(number):
-            within = lax.rem(number, block_of(c))
-            q = within // capacity
-            row = q * group + (number // block_of(c)) * capacity + lax.rem(within, capacity)
-            return jnp.where(within < CHUNK_PIECES[c] * capacity, row, -1)
-
-        shape = (CHUNK_PIECES[c] * group, chips * block_of(c))
-        unpack[c][...] = hot(iota(shape, 0) == place_of(iota((1, shape[1]), 1)))
-        repack[c][...] = hot(iota(shape[::-1], 1) == place_of(iota((shape[1], 1), 0)))
-    shape = (group, chips * slots)
-    wanted = iota((group, 1), 0)
-    wanted = (wanted // capacity) * slots + lax.rem(wanted, capacity)
-    slot_pick[...] = hot(iota(shape, 1) == wanted)
 
     earlier = hot(iota((tokens, tokens), 0) < iota((tokens, tokens), 1))
     for m in range(micro_count):
@@ -217,6 +202,23 @@
 
     pl.semaphore_wait(barrier, 2 * (chips - 1) + 1 + 2)
 
+    def build_matrices():
+        for c in range(CHUNKS):
+
+            def place_of(number):
+                within = lax.rem(number, block_of(c))
+                q = within // capacity
+                row = q * half_group + (number // block_of(c)) * capacity + lax.rem(within, capacity)
+                return jnp.where(within < CHUNK_PIECES[c] * capacity, row, -1)
+
+            shape = (CHUNK_PIECES[c] * half_group, half_chips * block_of(c))
+            unpack[c][...] = hot(iota(shape, 0) == place_of(iota((1, shape[1]), 1)))
+            repack[c][...] = hot(iota(shape[::-1], 1) == place_of(iota((shape[1], 1), 0)))
+        shape = (group, chips * slots)
+        wanted = iota((group, 1), 0)
+        wanted = (wanted // capacity) * slots + lax.rem(wanted, capacity)
+        slot_pick[...] = hot(iota(shape, 1) == wanted)
+
     def wait_all(buffer, semaphore):
         pltpu.make_async_copy(buffer, buffer, semaphore).wait()
 
@@ -262,12 +264,16 @@
         ]
 
     def unpack_rows(source, m, c, way, part):
-        rows = matmul(unpack[c][...], source[m].reshape(chips * block_of(c), piece))
+        rows = [
+            matmul(unpack[c][...], blocks.reshape(half_chips * block_of(c), piece))
+            for blocks in (source[m, :half_chips], source[m, half_chips:])
+        ]
         mine = slice(part * group, (part + 1) * group)
         square = jnp.zeros((group, piece), f32)
         for q in range(CHUNK_PIECES[c]):
             at = slice(begin_of(c, q), begin_of(c, q + 1))
-            found = rows[q * group : (q + 1) * group]
+            found = [half[q * half_group : (q + 1) * half_group] for half in rows]
+            found = jnp.concatenate(found, axis=0)
             if way == 0:
                 square += found * found
                 found = found * gain_ref[:, at]
@@ -323,9 +329,15 @@
         for c in range(CHUNKS):
             copies[c].wait()
             total = half_own[c][...].astype(f32) + half_recv[way][c][m].astype(f32)
-            total = total.astype(bf16).reshape(CHUNK_PIECES[c] * group, piece)
+            packed = [
+                matmul(
+                    repack[c][...],
+                    half.reshape(CHUNK_PIECES[c] * half_group, piece).astype(bf16),
+                )
+                for half in (total[:, :half_group], total[:, half_group:])
+            ]
             post(
-                matmul(repack[c][...], total),
+                jnp.concatenate(packed, axis=0),
                 m,
                 c,
                 combine_send[way][c],
@@ -402,6 +414,7 @@
     def forward_expert(m):
         @pl.when(m == 0)
         def _():
+            build_matrices()
             for copy in weights:
                 copy.wait()
 
@@ -627,10 +640,10 @@
         return (chunks, chunks) if ways else chunks
 
     def rows_of(c):
-        return CHUNK_PIECES[c] * group
+        return CHUNK_PIECES[c] * group // 2
 
     def blocks_of(c):
-        return chips * block_rows(c, capacity)
+        return chips * block_rows(c, capacity) // 2
 
     def lanes_of(c):
         return CHUNK_PIECES[c] * tokens

time: 318 us -> 308 us (0.969)
  Pallas kernels: 312 us -> 302 us
    pallas_call x1, Pallas kernels: 312 us -> 302 us  [on_device(): pl.pallas_call(functools.partial(relay_kernel, geometry), out_shape=(out,...]
where the time goes in v5:
time: 308 us; the launch traced here: 307 us
  Pallas kernels  302 us (98%)
  local copies, waits for them, and re-layouts  4.32 us (1%)
    pallas_call x1, Pallas kernels, on_device(): pl.pallas_call(functools.partial(relay_kernel, geometry), out_shape=(out,...  302 us

profile of v5, /device:TPU:1, one launch (start us, length us, event | category | flops | bytes accessed | tf_op | source)
XLA Modules:
  0.0 307.3 jit_solution(9162807731336757642)
XLA Ops:
  0.6 302.3 %shard_map.95 = (bf16[4,32,3584]{2,1,0:T(8,128)(2,1)}, bf16[4,32,3584]{2,1,0:T(8,128)(2,1)}) custom-call(bf16[4,32,3584]{2,1,0:T(8,128)(2,1)} %inputs_ref.1, bf16[4,32,3584]{2,1,0:T(8,128)(2,1)} %cotangent_ref.1, f32[1,3584]{1,0:T(1,128)} %gain_ref.1, bf16[16,3584]{1,0:T(8,128)(2,1)} %bitcast.16, bf16[3584,512]{1,0:T(8,128)(2,1)} %bitcast.11, ...), custom_call_target="tpu_custom_call" | custom-call | tf_op jit(solution)/shard_map/pallas_call | solution.py:661
  303.0 2.2 copy.12
  305.1 2.2 copy.13

commit v6 on v5

--- a/solution.py
+++ b/solution.py
@@ -660,7 +660,7 @@
     parts = micro_count * CHUNKS
     forward_out, backward_out = pl.pallas_call(
         functools.partial(relay_kernel, geometry),
-        out_shape=(out, out),
+        out_shape=(pltpu.VMEM(out.shape, bf16),) * 2,
         in_specs=[anywhere] * 2 + [inside] * 2 + [anywhere] * 3 + [inside],
         out_specs=(inside, inside),
         scratch_shapes=[
@@ -709,7 +709,7 @@
             dma((micro_count, 2)),
         ],
         compiler_params=pltpu.CompilerParams(
-            collective_id=0, has_side_effects=True, vmem_limit_bytes=66_000_000
+            collective_id=0, has_side_effects=True, vmem_limit_bytes=62_500_000
         ),
     )(
         inputs,

time: 308 us -> 304 us (0.987)
  no operation moved by 1% of the time
where the time goes in v6:
time: 304 us
  Pallas kernels  301 us (99%)
    pallas_call x1, Pallas kernels, on_device(): pl.pallas_call(functools.partial(relay_kernel, geometry), out_shape=(pltp...  301 us

profile of v6, /device:TPU:1, one launch (start us, length us, event | category | flops | bytes accessed | tf_op | source)
XLA Modules:
  0.0 303.6 jit_solution(16525783975496625098)
XLA Ops:
  0.6 301.1 %shard_map.95 = (bf16[4,32,3584]{2,1,0:T(8,128)(2,1)S(1)}, bf16[4,32,3584]{2,1,0:T(8,128)(2,1)S(1)}) custom-call(bf16[4,32,3584]{2,1,0:T(8,128)(2,1)} %inputs_ref.1, bf16[4,32,3584]{2,1,0:T(8,128)(2,1)} %cotangent_ref.1, f32[1,3584]{1,0:T(1,128)} %gain_ref.1, bf16[16,3584]{1,0:T(8,128)(2,1)} %bitcast.16, bf16[3584,512]{1,0:T(8,128)(2,1)} %bitcast.13, ...), custom_call_target="tpu_custom_call" | custom-call | tf_op jit(solution)/shard_map/pallas_call | solution.py:661
  301.7 0.9 copy.12
  302.7 0.9 copy.13
